TPU v7x, 256 devices: a whole 4x4x8 slice. The times are simulated.
256 devices in a mesh: gx: 128 (over z, x, y), sa: 2 (over core).
Axes of the slice: x: 4, y: 4, z: 8, core: 2. Of those that a mesh axis runs over, the one named last changes fastest.
Arguments:
- inputs: bfloat16 [2, 16, 512, 128, 128], P('sa', None, 'gx'), may hold values from -6 to 6
- preact: bfloat16 [2, 16, 512, 128, 128], P('sa', None, 'gx'), may hold values from -6 to 6
- cotangent: bfloat16 [2, 16, 512, 128, 128], P('sa', None, 'gx'), may hold values from -6 to 6
- mode_weight: bfloat16 [16, 16, 2048, 128], P(None, None, 'gx'), may hold values from -1 to 1
- bypass_weight: bfloat16 [16, 16], replicated, may hold values from -1.5 to 1.5
Outputs:
- input_grad: bfloat16 [2, 16, 512, 128, 128], P('sa', None, 'gx')
- mode_grad: float32 [16, 16, 2048, 128], P(None, None, ('gx', 'sa'))
All inputs are finite; a program needn't handle non-finite values.
Results may differ from a plain program's by a relative error of at most 0.0097.
Values may be sent and summed in bfloat16 or wider, within the bound.
No kernel may reach another device: no remote copies, remote signals or barrier semaphores. Data moves between devices by JAX's collectives and lax.ppermute only.
A program may use at most 128 MiB of HBM per device.

v0:
```python
import math

import jax
import jax.numpy as jnp
import numpy as np
from jax import lax
from jax.experimental import pallas as pl
from jax.experimental.pallas import tpu as pltpu
from jax.sharding import PartitionSpec as P

MY = 64
MT = 32

root_half = math.sqrt(0.5)
gauss_norm = 1.0 / math.sqrt(2.0 * math.pi)
f32 = jnp.float32
bf16 = jnp.bfloat16


def tables(kept_count, length, two_sided):
    frequency = np.arange(kept_count)
    if two_sided:
        frequency = np.where(
            frequency < kept_count // 2, frequency, frequency + (length - kept_count)
        )
    product = frequency[:, None] * np.arange(length)[None, :] % length
    phase_angle = product * (2.0 * math.pi / length)
    return (
        np.cos(phase_angle).astype(np.float32).astype(bf16).astype(np.float32),
        np.sin(phase_angle).astype(np.float32).astype(bf16).astype(np.float32),
    )


def constants(cells_x, cells_y, cells_time, modes_x, slab):
    ct, st = tables(MT, cells_time, False)
    cy, sy = tables(MY, cells_y, True)
    cx, sx = tables(modes_x, cells_x, True)
    four = np.eye(4, dtype=np.float32)
    time = np.stack([ct, -st]).reshape(2, 2, MT // 2, cells_time)
    time_forward = np.einsum("cd,qhkt->ctqhdk", four, time).reshape(4 * cells_time, -1)
    time_inverse = np.einsum("cd,qhkt->qhckdt", four, time).reshape(-1, 4 * cells_time)
    plane = np.block([[cy, sy], [-sy, cy]])
    x_forward = np.stack([np.concatenate([cx, -sx]).T, np.concatenate([sx, cx]).T], 1)
    devices = cells_x // slab
    both = np.einsum(
        "fg,dvr->frdgv", np.eye(2, dtype=np.float32), x_forward.reshape(devices, 2 * slab, -1)
    ).reshape(2 * 2 * modes_x, -1)
    x_inverse = np.stack([np.concatenate([cx, -sx]), np.concatenate([sx, cx])], -1)
    x_inverse = x_inverse.reshape(2 * modes_x, -1).T
    return [
        a.astype(bf16) for a in (time_forward, time_inverse, plane, plane.T, both, x_inverse)
    ]


def low_lanes(shape):
    return lax.broadcasted_iota(jnp.int32, shape, len(shape) - 1) < 64


def gelu_backward(values, cotangent):
    slope = (
        0.5 * (1.0 + lax.erf(values * root_half))
        + values * jnp.exp(-0.5 * values * values) * gauss_norm
    )
    return cotangent * slope


def forward_kernel(pre_ref, cot_ref, inp_ref, time_ref, plane_ref, send_ref, dz_ref, acc0, acc1):
    x = pl.program_id(0)
    for c in range(16):
        dz_ref[c] = gelu_backward(pre_ref[c].astype(f32), cot_ref[c].astype(f32)).astype(bf16)
    low = low_lanes((128, 128))
    for field, ref in enumerate((dz_ref, inp_ref)):
        rows = jnp.concatenate(
            [jnp.concatenate([ref[4 * g + c] for c in range(4)], axis=1) for g in range(4)], axis=0
        )
        sect = jnp.dot(rows, time_ref[...], preferred_element_type=f32).astype(bf16)
        stacked = jnp.concatenate(
            [
                jnp.concatenate(
                    [sect[128 * g : 128 * g + 128, 128 * q : 128 * q + 128] for g in range(4)],
                    axis=1,
                )
                for q in range(2)
            ],
            axis=0,
        )
        plane = jnp.dot(plane_ref[...], stacked, preferred_element_type=f32)
        for pair, acc in enumerate((acc0, acc1)):
            first = plane[:, 256 * pair : 256 * pair + 128]
            second = plane[:, 256 * pair + 128 : 256 * pair + 256]
            halves = (
                jnp.where(low, first, pltpu.roll(second, 64, 1)),
                jnp.where(low, pltpu.roll(first, 64, 1), second),
            )
            for h in range(2):
                for a in range(2):
                    start = h * 16 + field * 8 + a + 2 * x
                    acc[pl.ds(start, 64, stride=32), :] = halves[h][64 * a : 64 * a + 64]

    @pl.when(x == 3)
    def _():
        send_ref[:, :, 0:128] = acc0[...].reshape(128, 16, 128).astype(bf16)
        send_ref[:, :, 128:256] = acc1[...].reshape(128, 16, 128).astype(bf16)


def middle_kernel(scale_in, scale_out):
    def kernel(core_ref, recv_ref, xf_ref, w_ref, xi_ref, send_ref, mine_ref, other_ref, back_ref, g_ref, gr_ref):
        core = core_ref[0]
        block = recv_ref[...].reshape(2048, 256)
        summed = jnp.dot(xf_ref[...], block, preferred_element_type=f32).T
        hats = jnp.concatenate([summed[:, :128] * scale_out, summed[:, 128:] * scale_in], axis=1)
        hats = hats.astype(bf16).astype(f32)
        grad = hats[:, :128]
        g_ref[0] = grad
        g_ref[1] = hats[:, 128:]
        gr_ref[...] = pltpu.roll(grad, 64, 1)
        for f in range(2):
            for c in range(16):
                mine_ref[f, c] = g_ref[f, pl.ds(16 * c + 8 * core, 8), :].astype(bf16)
                other_ref[f, c] = g_ref[f, pl.ds(16 * c + 8 - 8 * core, 8), :].astype(bf16)
        low = low_lanes((16, 128))
        for i in range(16):
            same = jnp.zeros((16, 128), f32)
            cross = jnp.zeros((16, 128), f32)
            for o in range(16):
                weight = w_ref[i, o].astype(f32)
                same = same + weight * g_ref[0, 16 * o : 16 * o + 16, :]
                cross = cross + weight * gr_ref[16 * o : 16 * o + 16, :]
            back = jnp.where(low, same + pltpu.roll(same, 64, 1), pltpu.roll(cross, 64, 1) - cross)
            back_ref[16 * i : 16 * i + 16, :] = back.astype(bf16)
        grid_rows = lax.dot_general(
            xi_ref[...], back_ref[...], (((1,), (1,)), ((), ())), preferred_element_type=f32
        )
        send_ref[...] = grid_rows.reshape(128, 8, 256).astype(bf16)

    return kernel


def mode_kernel(mine_ref, other_ref, out_ref, g_ref, gx_ref):
    low = low_lanes((16, 8, 128))
    for s, ref in enumerate((mine_ref, other_ref)):
        grad = ref[0].astype(f32)
        rolled = pltpu.roll(grad, 64, 2)
        g_ref[s] = grad
        gx_ref[s] = jnp.where(low, rolled, -rolled)
    low = low_lanes((8, 128))
    for i in range(16):
        real, imag = [], []
        for ref in (mine_ref, other_ref):
            value = ref[1, i].astype(f32)
            rolled = pltpu.roll(value, 64, 1)
            real.append(jnp.where(low, value, rolled))
            imag.append(jnp.where(low, rolled, value))
        for o in range(16):
            out_ref[i, o] = (
                real[0] * g_ref[0, o]
                + imag[0] * gx_ref[0, o]
                + (real[1] * g_ref[1, o] + imag[1] * gx_ref[1, o])
            )


def bypass_kernel(b_ref, dz_ref, out_ref):
    row = lax.broadcasted_iota(jnp.int32, (256, 16), 0)
    col = lax.broadcasted_iota(jnp.int32, (256, 16), 1)
    spread = jnp.where(row // 16 == col, 1.0, 0.0).astype(bf16)
    left = jnp.dot(spread, b_ref[...], preferred_element_type=f32).astype(bf16)
    full = lax.dot_general(left, spread, (((1,), (1,)), ((), ())), preferred_element_type=f32)
    row = lax.broadcasted_iota(jnp.int32, (256, 256), 0)
    col = lax.broadcasted_iota(jnp.int32, (256, 256), 1)
    mix = jnp.where(row % 16 == col % 16, full, 0.0).astype(bf16)
    rows = jnp.concatenate(
        [
            jnp.concatenate([dz_ref[o, 16 * b : 16 * b + 16, :] for o in range(16)], axis=0)
            for b in range(8)
        ],
        axis=1,
    )
    mixed = jnp.dot(mix, rows, preferred_element_type=f32)
    for i in range(16):
        for b in range(8):
            out_ref[i, 16 * b : 16 * b + 16, :] = mixed[
                16 * i : 16 * i + 16, 128 * b : 128 * b + 128
            ]


def inverse_kernel(scale_in):
    def kernel(recv_ref, plane_ref, time_ref, bypass_ref, out_ref, rows_ref):
        x = pl.program_id(0)

        @pl.when(x == 0)
        def _():
            block = recv_ref[...].astype(f32).reshape(64, 2, 8, 256)
            low = low_lanes((512, 128))
            for v in range(2):
                first = block[:, 0, :, 128 * v : 128 * v + 128].reshape(512, 128)
                second = block[:, 1, :, 128 * v : 128 * v + 128].reshape(512, 128)
                rows_ref[2 * v] = jnp.where(low, first, pltpu.roll(second, 64, 1))
                rows_ref[2 * v + 1] = jnp.where(low, pltpu.roll(first, 64, 1), second)

        spectra = jnp.concatenate(
            [
                jnp.concatenate(
                    [rows_ref[g, pl.ds(2 * x + a, 64, stride=8), :] for a in range(2)], axis=0
                )
                for g in range(4)
            ],
            axis=1,
        ).astype(bf16)
        joined = jnp.dot(plane_ref[...], spectra, preferred_element_type=f32).astype(bf16)
        stacked = jnp.concatenate(
            [
                jnp.concatenate(
                    [joined[128 * q : 128 * q + 128, 128 * g : 128 * g + 128] for q in range(2)],
                    axis=1,
                )
                for g in range(4)
            ],
            axis=0,
        )
        spectral = jnp.dot(stacked, time_ref[...], preferred_element_type=f32)
        for g in range(4):
            for c in range(4):
                out_ref[4 * g + c] = (
                    scale_in * spectral[128 * g : 128 * g + 128, 128 * c : 128 * c + 128]
                    + bypass_ref[4 * g + c]
                ).astype(bf16)

    return kernel


def whole(*shape):
    return pl.BlockSpec(shape, lambda *_: (0,) * len(shape))


def per_cell():
    return pl.BlockSpec((16, None, 128, 128), lambda x: (0, x, 0, 0))


def shards(inputs, preact, cotangent, mode_weight, bypass_weight):
    slab = inputs.shape[2]
    cells_y = inputs.shape[3]
    cells_time = inputs.shape[4]
    cells_x = slab * lax.axis_size("gx")
    modes_x = mode_weight.shape[3] // 2
    cell_count = cells_x * cells_y * cells_time
    scale_in = float(modes_x * MY * MT * cell_count) ** (-0.25)
    scale_out = float(cell_count) ** (-0.5)
    time_forward, time_inverse, plane, plane_back, x_forward, x_inverse = constants(
        cells_x, cells_y, cells_time, modes_x, slab
    )
    core = lax.axis_index("sa").astype(jnp.int32).reshape(1)

    send, dz = pl.pallas_call(
        forward_kernel,
        grid=(4,),
        in_specs=[per_cell(), per_cell(), per_cell(), whole(512, 256), whole(128, 256)],
        out_specs=[whole(128, 16, 256), per_cell()],
        out_shape=[
            jax.ShapeDtypeStruct((128, 16, 256), bf16),
            jax.ShapeDtypeStruct((16, 4, 128, 128), bf16),
        ],
        scratch_shapes=[pltpu.VMEM((2048, 128), f32), pltpu.VMEM((2048, 128), f32)],
        name="forward",
    )(preact[0], cotangent[0], inputs[0], time_forward, plane)
    recv = lax.all_to_all(send, "gx", split_axis=0, concat_axis=0, tiled=True)
    bypass = pl.pallas_call(
        bypass_kernel,
        grid=(4,),
        in_specs=[whole(16, 16), per_cell()],
        out_specs=per_cell(),
        out_shape=jax.ShapeDtypeStruct((16, 4, 128, 128), f32),
        name="bypass",
    )(bypass_weight, dz)
    rows, mine, other = pl.pallas_call(
        middle_kernel(scale_in, scale_out),
        in_specs=[pl.BlockSpec(memory_space=pltpu.SMEM)]
        + [pl.BlockSpec(memory_space=pltpu.VMEM)] * 4,
        out_specs=[pl.BlockSpec(memory_space=pltpu.VMEM)] * 3,
        out_shape=[
            jax.ShapeDtypeStruct((128, 8, 256), bf16),
            jax.ShapeDtypeStruct((2, 16, 8, 128), bf16),
            jax.ShapeDtypeStruct((2, 16, 8, 128), bf16),
        ],
        scratch_shapes=[
            pltpu.VMEM((256, 128), bf16),
            pltpu.VMEM((2, 256, 128), f32),
            pltpu.VMEM((256, 128), f32),
        ],
        name="middle",
    )(core, recv, x_forward, mode_weight, x_inverse)
    back = lax.all_to_all(rows, "gx", split_axis=0, concat_axis=0, tiled=True)
    theirs = lax.ppermute(other, "sa", [(0, 1), (1, 0)])
    mode_grad = pl.pallas_call(
        mode_kernel,
        out_shape=jax.ShapeDtypeStruct((16, 16, 8, 128), f32),
        scratch_shapes=[pltpu.VMEM((2, 16, 8, 128), f32), pltpu.VMEM((2, 16, 8, 128), f32)],
        name="modes",
    )(mine, theirs)
    input_grad = pl.pallas_call(
        inverse_kernel(scale_in),
        grid=(4,),
        in_specs=[whole(128, 8, 256), whole(256, 128), whole(256, 512), per_cell()],
        out_specs=per_cell(),
        out_shape=jax.ShapeDtypeStruct((16, 4, 128, 128), bf16),
        scratch_shapes=[pltpu.VMEM((4, 512, 128), f32)],
        name="inverse",
    )(back, plane_back, time_inverse, bypass)
    return (input_grad[None], mode_grad)


def solution(mesh):
    field = P("sa", None, "gx", None, None)
    return jax.shard_map(
        shards,
        mesh=mesh,
        in_specs=(field, field, field, P(None, None, "gx", None), P()),
        out_specs=(field, P(None, None, ("gx", "sa"), None)),
        check_vma=False,
    )
```

profile of v0, /device:TPU:2, one launch (start us, length us, event | category | flops | bytes accessed | tf_op | source)
XLA Modules:
  0.0 94.0 jit_solution(3093450061915142967)
XLA Ops:
  0.6 9.6 %forward.1 = (bf16[128,16,256]{2,1,0:T(8,128)(2,1)}, bf16[16,4,128,128]{3,2,1,0:T(8,128)(2,1)}) custom-call(bf16[16,4,128,128]{3,2,1,0:T(8,128)(2,1)} %bitcast.5, bf16[16,4,128,128]{3,2,1,0:T(8,128)(2,1)} %bitcast.6, bf16[16,4,128,128]{3,2,1,0:T(8,128)(2,1)} %bitcast.7, bf16[512,256]{1,0:T(8,128)(2,1)} %constant.16.clone.time_ref, ...), custom_call_target="tpu_custom_call" | custom-call | tf_op jit(solution)/shard_map/forward/pallas_call | solution.py:253
  10.2 15.4 %all-to-all-start = ((bf16[128,16,256]{2,1,0:T(8,128)(2,1)}), bf16[128,16,256]{2,1,0:T(8,128)(2,1)S(1)}, u32[]{:S(2)}, u32[]{:S(2)}) async-start(bf16[128,16,256]{2,1,0:T(8,128)(2,1)} %get-tuple-element.7), calls=%async_computation | async-start | bytes 2097152 | tf_op jit(solution)/shard_map/all_to_all | solution.py:265
  25.7 30.8 %all-to-all-done.recv_ref = bf16[128,16,256]{2,1,0:T(8,128)(2,1)S(1)} async-done(((bf16[128,16,256]{2,1,0:T(8,128)(2,1)}), bf16[128,16,256]{2,1,0:T(8,128)(2,1)S(1)}, u32[]{:S(2)}, u32[]{:S(2)}) %all-to-all-start) | async-done | bytes 1048608 | tf_op jit(solution)/shard_map/all_to_all | solution.py:265
  56.5 0.0 copy-start
  56.5 1.0 %copy-done = bf16[128,16,256]{2,1,0:T(8,128)(2,1)} copy-done((bf16[128,16,256]{2,1,0:T(8,128)(2,1)}, bf16[128,16,256]{2,1,0:T(8,128)(2,1)S(1)}, u32[]{:S(2)}) %copy-start) | copy-done | bytes 1048600
  57.5 4.2 %middle.1 = (bf16[128,8,256]{2,1,0:T(8,128)(2,1)}, bf16[2,16,8,128]{3,2,1,0:T(8,128)(2,1)}, bf16[2,16,8,128]{3,2,1,0:T(8,128)(2,1)}) custom-call(s32[1]{0:T(128)} %bitcast.core_ref, bf16[128,16,256]{2,1,0:T(8,128)(2,1)} %copy-done, bf16[256,2048]{1,0:T(8,128)(2,1)} %constant.18.clone.xf_ref, bf16[16,16,16,128]{3,2,1,0:T(8,128)(2,1)} %w_ref.1, ...), custom_call_target="tpu_custom_call" | custom-call | tf_op jit(solution)/shard_map/middle/pallas_call | solution.py:274
  61.7 6.5 %all-to-all-start.1 = ((bf16[128,8,256]{2,1,0:T(8,128)(2,1)}), bf16[128,8,256]{2,1,0:T(8,128)(2,1)S(1)}, u32[]{:S(2)}, u32[]{:S(2)}) async-start(bf16[128,8,256]{2,1,0:T(8,128)(2,1)} %get-tuple-element.8), calls=%async_computation.1 | async-start | bytes 1048576 | tf_op jit(solution)/shard_map/all_to_all | solution.py:291
  68.1 0.1 collective-permute-start
  68.2 5.1 %bypass.1.bypass_ref = f32[16,4,128,128]{3,2,1,0:T(8,128)} custom-call(bf16[16,16]{1,0:T(8,128)(2,1)} %b_ref.1, bf16[16,4,128,128]{3,2,1,0:T(8,128)(2,1)} %get-tuple-element.9.dz_ref), custom_call_target="tpu_custom_call" | custom-call | tf_op jit(solution)/shard_map/bypass/pallas_call | solution.py:266
  73.4 0.0 collective-permute-done.other_ref
  73.4 0.0 copy-start.2
  73.4 0.6 copy-done.2
  74.0 2.2 %modes.1 = f32[16,16,8,128]{3,2,1,0:T(8,128)} custom-call(bf16[2,16,8,128]{3,2,1,0:T(8,128)(2,1)} %get-tuple-element.10.mine_ref, bf16[2,16,8,128]{3,2,1,0:T(8,128)(2,1)} %copy-done.2), custom_call_target="tpu_custom_call" | custom-call | tf_op jit(solution)/shard_map/modes/pallas_call | solution.py:293
  76.2 11.5 %all-to-all-done.1.recv_ref = bf16[128,8,256]{2,1,0:T(8,128)(2,1)S(1)} async-done(((bf16[128,8,256]{2,1,0:T(8,128)(2,1)}), bf16[128,8,256]{2,1,0:T(8,128)(2,1)S(1)}, u32[]{:S(2)}, u32[]{:S(2)}) %all-to-all-start.1) | async-done | bytes 524320 | tf_op jit(solution)/shard_map/all_to_all | solution.py:291
  87.7 0.0 copy-start.1
  87.7 0.8 copy-done.1
  88.5 5.5 %inverse.1 = bf16[16,4,128,128]{3,2,1,0:T(8,128)(2,1)} custom-call(bf16[128,8,256]{2,1,0:T(8,128)(2,1)} %copy-done.1, bf16[256,128]{1,0:T(8,128)(2,1)} %constant.20.clone.plane_ref, bf16[256,512]{1,0:T(8,128)(2,1)} %constant.21.clone.time_ref, f32[16,4,128,128]{3,2,1,0:T(8,128)} %bypass.1.bypass_ref), custom_call_target="tpu_custom_call" | custom-call | tf_op jit(solution)/shard_map/inverse/pallas_call | solution.py:299
Async XLA Ops:
  10.2 46.3 %all-to-all-start = ((bf16[128,16,256]{2,1,0:T(8,128)(2,1)}), bf16[128,16,256]{2,1,0:T(8,128)(2,1)S(1)}, u32[]{:S(2)}, u32[]{:S(2)}) async-start(bf16[128,16,256]{2,1,0:T(8,128)(2,1)} %get-tuple-element.7), calls=%async_computation | async-start | bytes 2097152 | tf_op jit(solution)/shard_map/all_to_all | solution.py:265
  56.5 1.0 %copy-start = (bf16[128,16,256]{2,1,0:T(8,128)(2,1)}, bf16[128,16,256]{2,1,0:T(8,128)(2,1)S(1)}, u32[]{:S(2)}) copy-start(bf16[128,16,256]{2,1,0:T(8,128)(2,1)S(1)} %all-to-all-done.recv_ref) | copy-start | bytes 3145732
  61.7 26.0 %all-to-all-start.1 = ((bf16[128,8,256]{2,1,0:T(8,128)(2,1)}), bf16[128,8,256]{2,1,0:T(8,128)(2,1)S(1)}, u32[]{:S(2)}, u32[]{:S(2)}) async-start(bf16[128,8,256]{2,1,0:T(8,128)(2,1)} %get-tuple-element.8), calls=%async_computation.1 | async-start | bytes 1048576 | tf_op jit(solution)/shard_map/all_to_all | solution.py:291
  68.1 5.2 %collective-permute-start = (bf16[2,16,8,128]{3,2,1,0:T(8,128)(2,1)}, bf16[2,16,8,128]{3,2,1,0:T(8,128)(2,1)S(1)}, u32[]{:S(2)}, u32[]{:S(2)}) collective-permute-start(bf16[2,16,8,128]{3,2,1,0:T(8,128)(2,1)} %get-tuple-element.11), channel_id=1, source_target_pairs={{0,1},{1,0},{2,3},{3,2},{4,5},{5,4},{6,7},{7,6},{8,9},{9,8},{10,11... | collective-permute-start | bytes 196616 | tf_op jit(solution)/shard_map/ppermute | solution.py:292
  73.4 0.6 copy-start.2
  87.7 0.8 copy-start.1
where the time goes:
time: 94.4 us; the launch traced here: 94 us
  waiting for transfers between devices  42.3 us (45%)
  Pallas kernels  26.6 us (28%)
  starting transfers between devices  22 us (23%)
  local copies, waits for them, and re-layouts  2.41 us (3%)
    all_to_all x1, waiting for transfers between devices, shards(): recv = lax.all_to_all(send, 'gx', split_axis=0, concat_axis=0, tiled=True)  30.8 us
    all_to_all x1, starting transfers between devices, shards(): recv = lax.all_to_all(send, 'gx', split_axis=0, concat_axis=0, tiled=True)  15.4 us
    all_to_all x1, waiting for transfers between devices, shards(): back = lax.all_to_all(rows, 'gx', split_axis=0, concat_axis=0, tiled=True)  11.5 us
    pallas_call x1, Pallas kernels, shards(): pl.pallas_call(forward_kernel, grid=(4,), in_specs=[per_cell(), per_cell(...  9.58 us
    all_to_all x1, starting transfers between devices, shards(): back = lax.all_to_all(rows, 'gx', split_axis=0, concat_axis=0, tiled=True)  6.48 us
    pallas_call x1, Pallas kernels, shards(): pl.pallas_call(inverse_kernel(scale_in), grid=(4,), in_specs=[whole(128,...  5.48 us
    pallas_call x1, Pallas kernels, shards(): pl.pallas_call(bypass_kernel, grid=(4,), in_specs=[whole(16, 16), per_cel...  5.14 us
    pallas_call x1, Pallas kernels, shards(): pl.pallas_call(middle_kernel(scale_in, scale_out), in_specs=[pl.BlockSpec...  4.19 us
  transfers between devices with their start and end apart: 3, of which 2 were waited for; matrix products, arithmetic and copies ran while one was open for 0% of the time, Pallas kernels for 8%

commit v1 on v0

v1 whole, which is shorter than its diff:
```python
import math

import jax
import jax.numpy as jnp
import numpy as np
from jax import lax
from jax.experimental import pallas as pl
from jax.experimental.pallas import tpu as pltpu
from jax.sharding import PartitionSpec as P

MY = 64
MT = 32

root_half = math.sqrt(0.5)
gauss_norm = 1.0 / math.sqrt(2.0 * math.pi)
f32 = jnp.float32
bf16 = jnp.bfloat16


def tables(kept_count, length, two_sided):
    frequency = np.arange(kept_count)
    if two_sided:
        frequency = np.where(
            frequency < kept_count // 2, frequency, frequency + (length - kept_count)
        )
    product = frequency[:, None] * np.arange(length)[None, :] % length
    phase_angle = product * (2.0 * math.pi / length)
    return (
        np.cos(phase_angle).astype(np.float32).astype(bf16).astype(np.float32),
        np.sin(phase_angle).astype(np.float32).astype(bf16).astype(np.float32),
    )


def constants(cells_x, cells_y, cells_time, modes_x, slab):
    ct, st = tables(MT, cells_time, False)
    cy, sy = tables(MY, cells_y, True)
    cx, sx = tables(modes_x, cells_x, True)
    four = np.eye(4, dtype=np.float32)
    time = np.stack([ct, -st]).reshape(2, 2, MT // 2, cells_time)
    time_forward = np.einsum("cd,qhkt->ctqhdk", four, time).reshape(4 * cells_time, -1)
    time_inverse = np.einsum("cd,qhkt->qhckdt", four, time).reshape(-1, 4 * cells_time)
    plane = np.block([[cy, sy], [-sy, cy]])
    plane_rows = plane.reshape(2, MY, 1, -1).repeat(slab, 2).transpose(1, 2, 0, 3)
    plane_rows = plane_rows.reshape(MY * slab * 2, -1)
    line = np.stack([np.concatenate([cx, -sx]), np.concatenate([sx, cx])], -1)
    line = line.reshape(2 * modes_x, -1).T
    return [
        a.astype(bf16) for a in (time_forward, time_inverse, plane_rows, plane.T, line)
    ]


def low_lanes(shape):
    return lax.broadcasted_iota(jnp.int32, shape, len(shape) - 1) < 64


def gelu_backward(values, cotangent):
    scaled = values * root_half
    density = jnp.exp2((scaled * scaled) * -math.log2(math.e))
    slope = (1.0 + lax.erf(scaled)) + (scaled * (4.0 * root_half * gauss_norm)) * density
    return (cotangent * 0.5) * slope


def forward_kernel(
    pre_hbm,
    cot_hbm,
    inp_hbm,
    time_hbm,
    plane_hbm,
    send_hbm,
    dz_ref,
    pre_ref,
    cot_ref,
    inp_ref,
    time_ref,
    plane_ref,
    send_ref,
    table_ref,
    sect_ref,
    half_ref,
    sems,
    table_sems,
    sent,
):
    plane_copy = pltpu.make_async_copy(plane_hbm, plane_ref, table_sems.at[0])
    time_copy = pltpu.make_async_copy(time_hbm, time_ref, table_sems.at[1])
    plane_copy.start()
    time_copy.start()
    copies = []
    for g in range(4):
        part = pl.ds(4 * g, 4)
        trio = [
            pltpu.make_async_copy(src.at[part], dst.at[part], sems.at[n, g])
            for n, (src, dst) in enumerate(
                ((inp_hbm, inp_ref), (pre_hbm, pre_ref), (cot_hbm, cot_ref))
            )
        ]
        for copy in trio:
            copy.start()
        copies.append(trio)
    row_x = lax.broadcasted_iota(jnp.int32, (512, 256), 0) // 2 % 4
    plane_copy.wait()
    plane = plane_ref[...].astype(f32)
    for x in range(4):
        table_ref[:, 256 * x : 256 * x + 256] = jnp.where(row_x == x, plane, 0.0).astype(bf16)
    low = low_lanes((512, 128))
    time_copy.wait()

    def arrive(pair):
        for g in (2 * pair, 2 * pair + 1):
            for copy in copies[g]:
                copy.wait()

    def activation(g):
        for c in range(4 * g, 4 * g + 4):
            for x in range(4):
                dz_ref[c, x] = gelu_backward(
                    pre_ref[c, x].astype(f32), cot_ref[c, x].astype(f32)
                ).astype(bf16)

    def along_time(field, g):
        ref = (dz_ref, inp_ref)[field]
        rows = jnp.concatenate([ref[4 * g + c].reshape(512, 128) for c in range(4)], axis=1)
        sect = jnp.dot(rows, time_ref[...], preferred_element_type=f32).astype(bf16)
        side = g % 2
        for x in range(4):
            for q in range(2):
                sect_ref[
                    field,
                    256 * x + 128 * q : 256 * x + 128 * q + 128,
                    128 * side : 128 * side + 128,
                ] = sect[128 * x : 128 * x + 128, 128 * q : 128 * q + 128]

    def along_y(field):
        spectra = jnp.dot(table_ref[...], sect_ref[field], preferred_element_type=f32)
        first, second = spectra[:, :128], spectra[:, 128:]
        return (
            jnp.where(low, first, pltpu.roll(second, 64, 1)).reshape(64, 8, 128),
            jnp.where(low, pltpu.roll(first, 64, 1), second).reshape(64, 8, 128),
        )

    def hold(halves):
        for h in range(2):
            half_ref[h] = halves[h]

    def send(pair, halves):
        for h in range(2):
            both = jnp.concatenate([halves[h], half_ref[h]], axis=1)
            send_ref[:, h, :, 128 * pair : 128 * pair + 128] = both.astype(bf16)
        lanes = (slice(None), slice(None), slice(None), pl.ds(128 * pair, 128))
        copy = pltpu.make_async_copy(send_ref.at[lanes], send_hbm.at[lanes], sent.at[pair])
        copy.start()
        return copy

    arrive(0)
    along_time(1, 0)
    activation(0)
    along_time(1, 1)
    activation(1)
    hold(along_y(1))
    arrive(1)
    along_time(0, 0)
    along_time(0, 1)
    activation(2)
    first = send(0, along_y(0))
    along_time(1, 2)
    along_time(1, 3)
    activation(3)
    hold(along_y(1))
    along_time(0, 2)
    along_time(0, 3)
    second = send(1, along_y(0))
    first.wait()
    second.wait()


def middle_kernel(scale_in, scale_out):
    def kernel(
        core_ref,
        recv_ref,
        w_hbm,
        xi_ref,
        send_hbm,
        mine_ref,
        other_ref,
        w_ref,
        back_ref,
        g_ref,
        gr_ref,
        send_ref,
        loaded,
        sent,
    ):
        loads = [
            pltpu.make_async_copy(w_hbm.at[pl.ds(8 * n, 8)], w_ref.at[pl.ds(8 * n, 8)], loaded.at[n])
            for n in range(2)
        ]
        for load in loads:
            load.start()
        core = core_ref[0]
        line = xi_ref[...].T
        block = recv_ref[...].astype(f32)
        hats = []
        for f, scale in enumerate((scale_out, scale_in)):
            rows = block[:, 8 * f : 8 * f + 8, :].reshape(1024, 256).astype(bf16)
            summed = jnp.dot(line, rows, preferred_element_type=f32)
            hats.append((scale * summed).T.astype(bf16).astype(f32))
        grad = hats[0]
        g_ref[0] = grad
        g_ref[1] = hats[1]
        gr_ref[...] = pltpu.roll(grad, 64, 1)
        for f in range(2):
            for c in range(16):
                mine_ref[f, c] = g_ref[f, pl.ds(16 * c + 8 * core, 8), :].astype(bf16)
                other_ref[f, c] = g_ref[f, pl.ds(16 * c + 8 - 8 * core, 8), :].astype(bf16)
        low = low_lanes((16, 128))
        for i in range(16):
            if i % 8 == 0:
                loads[i // 8].wait()
            same = jnp.zeros((16, 128), f32)
            cross = jnp.zeros((16, 128), f32)
            for o in range(16):
                weight = w_ref[i, o].astype(f32)
                same = same + weight * g_ref[0, 16 * o : 16 * o + 16, :]
                cross = cross + weight * gr_ref[16 * o : 16 * o + 16, :]
            back = jnp.where(low, same + pltpu.roll(same, 64, 1), pltpu.roll(cross, 64, 1) - cross)
            back_ref[16 * i : 16 * i + 16, :] = back.astype(bf16)
        copies = []
        for part in range(2):
            grid_rows = lax.dot_general(
                xi_ref[512 * part : 512 * part + 512],
                back_ref[...],
                (((1,), (1,)), ((), ())),
                preferred_element_type=f32,
            )
            block = pl.ds(64 * part, 64)
            send_ref[block] = grid_rows.reshape(64, 8, 256).astype(bf16)
            copies.append(
                pltpu.make_async_copy(send_ref.at[block], send_hbm.at[block], sent.at[part])
            )
            copies[-1].start()
        for copy in copies:
            copy.wait()

    return kernel


def mode_kernel(mine_ref, other_ref, out_ref, g_ref, gx_ref):
    low = low_lanes((16, 8, 128))
    for s, ref in enumerate((mine_ref, other_ref)):
        grad = ref[0].astype(f32)
        rolled = pltpu.roll(grad, 64, 2)
        g_ref[s] = grad
        gx_ref[s] = jnp.where(low, rolled, -rolled)
    low = low_lanes((8, 128))
    for i in range(16):
        real, imag = [], []
        for ref in (mine_ref, other_ref):
            value = ref[1, i].astype(f32)
            rolled = pltpu.roll(value, 64, 1)
            real.append(jnp.where(low, value, rolled))
            imag.append(jnp.where(low, rolled, value))
        for o in range(16):
            out_ref[i, o] = (
                real[0] * g_ref[0, o]
                + imag[0] * gx_ref[0, o]
                + (real[1] * g_ref[1, o] + imag[1] * gx_ref[1, o])
            )


def bypass_kernel(
    b_ref, dz_ref, xi_hbm, out_hbm, xi_ref, out_ref, sems, sent
):
    copies = [
        pltpu.make_async_copy(src, dst, sems.at[n])
        for n, (src, dst) in enumerate(((xi_hbm, xi_ref),))
    ]
    for copy in copies:
        copy.start()
    row = lax.broadcasted_iota(jnp.int32, (256, 16), 0)
    col = lax.broadcasted_iota(jnp.int32, (256, 16), 1)
    spread = jnp.where(row // 16 == col, 1.0, 0.0).astype(bf16)
    left = jnp.dot(spread, b_ref[...], preferred_element_type=f32).astype(bf16)
    full = lax.dot_general(left, spread, (((1,), (1,)), ((), ())), preferred_element_type=f32)
    row = lax.broadcasted_iota(jnp.int32, (256, 256), 0)
    col = lax.broadcasted_iota(jnp.int32, (256, 256), 1)
    mix = jnp.where(row % 16 == col % 16, full, 0.0).astype(bf16)
    def cell(x, carry):
        rows = jnp.concatenate(
            [
                jnp.concatenate([dz_ref[o, x, 16 * b : 16 * b + 16, :] for o in range(16)], axis=0)
                for b in range(8)
            ],
            axis=1,
        )
        mixed = jnp.dot(mix, rows, preferred_element_type=f32)
        for i in range(16):
            for b in range(8):
                out_ref[i, x, 16 * b : 16 * b + 16, :] = mixed[
                    16 * i : 16 * i + 16, 128 * b : 128 * b + 128
                ]
        return carry

    lax.fori_loop(0, 4, cell, 0)
    copies.append(pltpu.make_async_copy(out_ref, out_hbm, sent))
    copies[-1].start()
    for copy in copies:
        copy.wait()


def inverse_kernel(scale_in):
    def kernel(recv_ref, plane_ref, time_ref, bypass_hbm, out_hbm, rows_ref, bypass_ref, out_ref, loads, sems):
        arriving = [
            pltpu.make_async_copy(bypass_hbm.at[:, x], bypass_ref.at[:, x], loads.at[x])
            for x in range(4)
        ]
        for copy in arriving:
            copy.start()
        block = recv_ref[...].astype(f32).reshape(64, 2, 8, 256)
        low = low_lanes((512, 128))
        for v in range(2):
            first = block[:, 0, :, 128 * v : 128 * v + 128].reshape(512, 128)
            second = block[:, 1, :, 128 * v : 128 * v + 128].reshape(512, 128)
            rows_ref[2 * v] = jnp.where(low, first, pltpu.roll(second, 64, 1))
            rows_ref[2 * v + 1] = jnp.where(low, pltpu.roll(first, 64, 1), second)
        copies = []
        for x in range(4):
            spectra = jnp.concatenate(
                [
                    jnp.concatenate(
                        [rows_ref[g, pl.ds(2 * x + a, 64, stride=8), :] for a in range(2)], axis=0
                    )
                    for g in range(4)
                ],
                axis=1,
            ).astype(bf16)
            joined = jnp.dot(plane_ref[...], spectra, preferred_element_type=f32).astype(bf16)
            stacked = jnp.concatenate(
                [
                    jnp.concatenate(
                        [
                            joined[128 * q : 128 * q + 128, 128 * g : 128 * g + 128]
                            for q in range(2)
                        ],
                        axis=1,
                    )
                    for g in range(4)
                ],
                axis=0,
            )
            arriving[x].wait()
            spectral = jnp.dot(stacked, time_ref[...], preferred_element_type=f32)
            for g in range(4):
                for c in range(4):
                    out_ref[4 * g + c, x] = (
                        scale_in * spectral[128 * g : 128 * g + 128, 128 * c : 128 * c + 128]
                        + bypass_ref[4 * g + c, x]
                    ).astype(bf16)
            copies.append(
                pltpu.make_async_copy(out_ref.at[:, x], out_hbm.at[:, x], sems.at[x])
            )
            copies[-1].start()
        for copy in copies:
            copy.wait()

    return kernel


def remote(array):
    return pltpu.with_memory_space_constraint(array, pltpu.HBM)


def local(array):
    return pltpu.with_memory_space_constraint(array, pltpu.VMEM)


def shards(inputs, preact, cotangent, mode_weight, bypass_weight):
    slab = inputs.shape[2]
    cells_y = inputs.shape[3]
    cells_time = inputs.shape[4]
    cells_x = slab * lax.axis_size("gx")
    modes_x = mode_weight.shape[3] // 2
    cell_count = cells_x * cells_y * cells_time
    scale_in = float(modes_x * MY * MT * cell_count) ** (-0.25)
    scale_out = float(cell_count) ** (-0.5)
    time_forward, time_inverse, plane, plane_back, line = constants(
        cells_x, cells_y, cells_time, modes_x, slab
    )
    core = lax.axis_index("sa").astype(jnp.int32).reshape(1)

    vmem = pl.BlockSpec(memory_space=pltpu.VMEM)
    hbm = pl.BlockSpec(memory_space=pltpu.HBM)
    field = (16, 4, 128, 128)
    send, dz = pl.pallas_call(
        forward_kernel,
        in_specs=[hbm] * 5,
        out_specs=[hbm, vmem],
        out_shape=[pltpu.HBM((64, 2, 16, 256), bf16), pltpu.VMEM(field, bf16)],
        scratch_shapes=[pltpu.VMEM(field, bf16)] * 3
        + [
            pltpu.VMEM(time_forward.shape, bf16),
            pltpu.VMEM(plane.shape, bf16),
            pltpu.VMEM((64, 2, 16, 256), bf16),
            pltpu.VMEM((512, 1024), bf16),
            pltpu.VMEM((2, 1024, 256), bf16),
            pltpu.VMEM((2, 64, 8, 128), f32),
            pltpu.SemaphoreType.DMA((3, 4)),
            pltpu.SemaphoreType.DMA((2,)),
            pltpu.SemaphoreType.DMA((2,)),
        ],
        name="forward",
        compiler_params=pltpu.CompilerParams(vmem_limit_bytes=24 << 20),
    )(
        remote(preact[0]),
        remote(cotangent[0]),
        remote(inputs[0]),
        remote(time_forward),
        remote(plane),
    )
    recv = lax.all_to_all(
        send.reshape(128, 16, 256), "gx", split_axis=0, concat_axis=0, tiled=True
    )
    bypass, line = pl.pallas_call(
        bypass_kernel,
        in_specs=[vmem, vmem, hbm],
        out_specs=[hbm, vmem],
        out_shape=[
            pltpu.HBM(field, f32),
            pltpu.VMEM(line.shape, bf16),
        ],
        scratch_shapes=[
            pltpu.VMEM(field, f32),
            pltpu.SemaphoreType.DMA((1,)),
            pltpu.SemaphoreType.DMA,
        ],
        name="bypass",
        compiler_params=pltpu.CompilerParams(vmem_limit_bytes=24 << 20),
    )(bypass_weight, local(dz), remote(line))
    rows, mine, other = pl.pallas_call(
        middle_kernel(scale_in, scale_out),
        in_specs=[pl.BlockSpec(memory_space=pltpu.SMEM), vmem, hbm, vmem],
        out_specs=[hbm, vmem, vmem],
        out_shape=[
            pltpu.HBM((128, 8, 256), bf16),
            pltpu.VMEM((2, 16, 8, 128), bf16),
            jax.ShapeDtypeStruct((2, 16, 8, 128), bf16),
        ],
        scratch_shapes=[
            pltpu.VMEM(mode_weight.shape, bf16),
            pltpu.VMEM((256, 128), bf16),
            pltpu.VMEM((2, 256, 128), f32),
            pltpu.VMEM((256, 128), f32),
            pltpu.VMEM((128, 8, 256), bf16),
            pltpu.SemaphoreType.DMA((2,)),
            pltpu.SemaphoreType.DMA((2,)),
        ],
        name="middle",
        compiler_params=pltpu.CompilerParams(vmem_limit_bytes=24 << 20),
    )(core, local(recv), remote(mode_weight), local(line))
    back = lax.all_to_all(rows, "gx", split_axis=0, concat_axis=0, tiled=True)
    theirs = lax.ppermute(other, "sa", [(0, 1), (1, 0)])
    mode_grad = pl.pallas_call(
        mode_kernel,
        in_specs=[vmem, vmem],
        out_specs=vmem,
        out_shape=jax.ShapeDtypeStruct((16, 16, 8, 128), f32),
        scratch_shapes=[pltpu.VMEM((2, 16, 8, 128), f32), pltpu.VMEM((2, 16, 8, 128), f32)],
        name="modes",
        compiler_params=pltpu.CompilerParams(vmem_limit_bytes=24 << 20),
    )(local(mine), local(theirs))
    input_grad = pl.pallas_call(
        inverse_kernel(scale_in),
        in_specs=[vmem, vmem, vmem, hbm],
        out_specs=hbm,
        out_shape=jax.ShapeDtypeStruct(field, bf16),
        scratch_shapes=[
            pltpu.VMEM((4, 512, 128), f32),
            pltpu.VMEM(field, f32),
            pltpu.VMEM(field, bf16),
            pltpu.SemaphoreType.DMA((4,)),
            pltpu.SemaphoreType.DMA((4,)),
        ],
        name="inverse",
        compiler_params=pltpu.CompilerParams(vmem_limit_bytes=24 << 20),
    )(local(back), local(plane_back), local(time_inverse), remote(bypass))
    return (input_grad[None], mode_grad)


def solution(mesh):
    field = P("sa", None, "gx", None, None)
    return jax.shard_map(
        shards,
        mesh=mesh,
        in_specs=(field, field, field, P(None, None, "gx", None), P()),
        out_specs=(field, P(None, None, ("gx", "sa"), None)),
        check_vma=False,
    )
```

time: 94.4 us -> 88.3 us (0.935)
  Pallas kernels: 26.6 us -> 19.9 us
  waiting for transfers between devices: 42.3 us -> 45.4 us
  local copies, waits for them, and re-layouts: 2.41 us -> 0.01 us
    all_to_all x1, waiting for transfers between devices: 11.5 us -> 16.9 us  [shards(): back = lax.all_to_all(rows, 'gx', split_axis=0, concat_axis=0, tiled=True)]
    pallas_call x4, Pallas kernels: 22.4 us -> 17.2 us  [the longest x1 8.87 us: shards(): pl.pallas_call(forward_kernel, in_specs=[hbm] * 5, out_specs=[hbm, vmem],...]
    all_to_all x1, waiting for transfers between devices: 30.8 us -> 27.3 us  [shards(): lax.all_to_all(send.reshape(128, 16, 256), 'gx', split_axis=0, concat_axi...]
    unnamed x6, local copies, waits for them, and re-layouts: 2.41 us -> 0.01 us
    pallas_call x1, Pallas kernels: 4.19 us -> 2.68 us  [shards(): pl.pallas_call(middle_kernel(scale_in, scale_out), in_specs=[pl.BlockSpec...]
    ppermute x1, waiting for transfers between devices: 0.01 us -> 1.24 us  [shards(): theirs = lax.ppermute(other, 'sa', [(0, 1), (1, 0)])]
  transfers between devices with their start and end apart: 3 -> 3, of which waited for: 2 -> 3; matrix products, arithmetic and copies ran while one was open for 0% -> 0% of each run, Pallas kernels for 8% -> 5%
where the time goes in v1:
time: 88.3 us; the launch traced here: 88.1 us
  waiting for transfers between devices  45.4 us (51%)
  starting transfers between devices  22 us (25%)
  Pallas kernels  19.9 us (23%)
    all_to_all x1, waiting for transfers between devices, shards(): lax.all_to_all(send.reshape(128, 16, 256), 'gx', split_axis=0, concat_axi...  27.3 us
    all_to_all x1, waiting for transfers between devices, shards(): back = lax.all_to_all(rows, 'gx', split_axis=0, concat_axis=0, tiled=True)  16.9 us
    all_to_all x1, starting transfers between devices, shards(): lax.all_to_all(send.reshape(128, 16, 256), 'gx', split_axis=0, concat_axi...  15.4 us
    pallas_call x1, Pallas kernels, shards(): pl.pallas_call(forward_kernel, in_specs=[hbm] * 5, out_specs=[hbm, vmem],...  8.87 us
    all_to_all x1, starting transfers between devices, shards(): back = lax.all_to_all(rows, 'gx', split_axis=0, concat_axis=0, tiled=True)  6.5 us
    pallas_call x1, Pallas kernels, shards(): pl.pallas_call(inverse_kernel(scale_in), in_specs=[vmem, vmem, vmem, hbm]...  3.51 us
    pallas_call x1, Pallas kernels, shards(): pl.pallas_call(bypass_kernel, in_specs=[vmem, vmem, hbm], out_specs=[hbm,...  3.5 us
    pallas_call x1, Pallas kernels, shards(): pl.pallas_call(middle_kernel(scale_in, scale_out), in_specs=[pl.BlockSpec...  2.68 us
  transfers between devices with their start and end apart: 3, of which 3 were waited for; matrix products, arithmetic and copies ran while one was open for 0% of the time, Pallas kernels for 5%

profile of v1, /device:TPU:2, one launch (start us, length us, event | category | flops | bytes accessed | tf_op | source)
XLA Modules:
  0.0 88.1 jit_solution(13384116812070500235)
XLA Ops:
  0.6 8.9 %forward.1 = (bf16[64,2,16,256]{3,2,1,0:T(8,128)(2,1)}, bf16[16,4,128,128]{3,2,1,0:T(8,128)(2,1)S(1)}) custom-call(bf16[16,4,128,128]{3,2,1,0:T(8,128)(2,1)} %bitcast.7, bf16[16,4,128,128]{3,2,1,0:T(8,128)(2,1)} %bitcast.8, bf16[16,4,128,128]{3,2,1,0:T(8,128)(2,1)} %bitcast.9, bf16[512,256]{1,0:T(8,128)(2,1)} %constant.14.clone.time_hbm, ...), custom_call_target="tpu_custom_call" | custom-call | tf_op jit(solution)/shard_map/forward/pallas_call | solution.py:393
  9.5 0.0 copy-start.2
  9.5 15.4 %all-to-all-start = ((bf16[128,16,256]{2,1,0:T(8,128)(2,1)}), bf16[128,16,256]{2,1,0:T(8,128)(2,1)S(1)}, u32[]{:S(2)}, u32[]{:S(2)}) async-start(bf16[128,16,256]{2,1,0:T(8,128)(2,1)} %bitcast.10), calls=%async_computation | async-start | bytes 2097152 | tf_op jit(solution)/shard_map/all_to_all | solution.py:419
  25.0 0.0 copy-done.2
  25.0 3.5 %bypass.1 = (f32[16,4,128,128]{3,2,1,0:T(8,128)}, bf16[1024,128]{1,0:T(8,128)(2,1)S(1)}) custom-call(bf16[16,16]{1,0:T(8,128)(2,1)S(1)} %copy-done.2, bf16[16,4,128,128]{3,2,1,0:T(8,128)(2,1)S(1)} %get-tuple-element.10.dz_ref, bf16[1024,128]{1,0:T(8,128)(2,1)} %constant.16.clone.xi_hbm), custom_call_target="tpu_custom_call" | custom-call | tf_op jit(solution)/shard_map/bypass/pallas_call | solution.py:422
  28.5 27.3 %all-to-all-done.recv_ref = bf16[128,16,256]{2,1,0:T(8,128)(2,1)S(1)} async-done(((bf16[128,16,256]{2,1,0:T(8,128)(2,1)}), bf16[128,16,256]{2,1,0:T(8,128)(2,1)S(1)}, u32[]{:S(2)}, u32[]{:S(2)}) %all-to-all-start) | async-done | bytes 1048608 | tf_op jit(solution)/shard_map/all_to_all | solution.py:419
  55.8 0.0 copy-start
  55.8 0.0 copy-start.1
  55.8 2.7 %middle.1 = (bf16[128,8,256]{2,1,0:T(8,128)(2,1)}, bf16[2,16,8,128]{3,2,1,0:T(8,128)(2,1)S(1)}, bf16[2,16,8,128]{3,2,1,0:T(8,128)(2,1)S(1)}) custom-call(s32[1]{0:T(128)} %bitcast.core_ref, bf16[128,16,256]{2,1,0:T(8,128)(2,1)S(1)} %all-to-all-done.recv_ref, bf16[16,16,16,128]{3,2,1,0:T(8,128)(2,1)} %w_hbm.1, bf16[1024,128]{1,0:T(8,128)(2,1)S(1)} %get-tuple-element.11.xi_ref), custom_call_target="tpu_custom_call" | custom-call | tf_op jit(solution)/shard_map/middle/pallas_call | solution.py:438
  58.5 6.5 %all-to-all-start.1 = ((bf16[128,8,256]{2,1,0:T(8,128)(2,1)}), bf16[128,8,256]{2,1,0:T(8,128)(2,1)S(1)}, u32[]{:S(2)}, u32[]{:S(2)}) async-start(bf16[128,8,256]{2,1,0:T(8,128)(2,1)} %get-tuple-element.12), calls=%async_computation.1 | async-start | bytes 1048576 | tf_op jit(solution)/shard_map/all_to_all | solution.py:459
  65.0 0.1 collective-permute-start
  65.1 1.2 %collective-permute-done.other_ref = bf16[2,16,8,128]{3,2,1,0:T(8,128)(2,1)S(1)} collective-permute-done((bf16[2,16,8,128]{3,2,1,0:T(8,128)(2,1)S(1)}, bf16[2,16,8,128]{3,2,1,0:T(8,128)(2,1)S(1)}, u32[]{:S(2)}, u32[]{:S(2)}) %collective-permute-start) | collective-permute-done | bytes 65568 | tf_op jit(solution)/shard_map/ppermute | solution.py:460
  66.4 1.3 %modes.1 = f32[16,16,8,128]{3,2,1,0:T(8,128)} custom-call(bf16[2,16,8,128]{3,2,1,0:T(8,128)(2,1)S(1)} %get-tuple-element.14.mine_ref, bf16[2,16,8,128]{3,2,1,0:T(8,128)(2,1)S(1)} %collective-permute-done.other_ref), custom_call_target="tpu_custom_call" | custom-call | tf_op jit(solution)/shard_map/modes/pallas_call | solution.py:461
  67.7 16.9 %all-to-all-done.1.recv_ref = bf16[128,8,256]{2,1,0:T(8,128)(2,1)S(1)} async-done(((bf16[128,8,256]{2,1,0:T(8,128)(2,1)}), bf16[128,8,256]{2,1,0:T(8,128)(2,1)S(1)}, u32[]{:S(2)}, u32[]{:S(2)}) %all-to-all-start.1) | async-done | bytes 524320 | tf_op jit(solution)/shard_map/all_to_all | solution.py:459
  84.6 0.0 copy-done
  84.6 0.0 copy-done.1
  84.6 3.5 %inverse.1 = bf16[16,4,128,128]{3,2,1,0:T(8,128)(2,1)} custom-call(bf16[128,8,256]{2,1,0:T(8,128)(2,1)S(1)} %all-to-all-done.1.recv_ref, bf16[256,128]{1,0:T(8,128)(2,1)S(1)} %copy-done.1, bf16[256,512]{1,0:T(8,128)(2,1)S(1)} %copy-done, f32[16,4,128,128]{3,2,1,0:T(8,128)} %get-tuple-element.13.bypass_hbm), custom_call_target="tpu_custom_call" | custom-call | tf_op jit(solution)/shard_map/inverse/pallas_call | solution.py:470
Async XLA Ops:
  9.5 15.5 %copy-start.2 = (bf16[16,16]{1,0:T(8,128)(2,1)S(1)}, bf16[16,16]{1,0:T(8,128)(2,1)}, u32[]{:S(2)}) copy-start(bf16[16,16]{1,0:T(8,128)(2,1)} %b_ref.1) | copy-start | bytes 1540
  9.5 46.3 %all-to-all-start = ((bf16[128,16,256]{2,1,0:T(8,128)(2,1)}), bf16[128,16,256]{2,1,0:T(8,128)(2,1)S(1)}, u32[]{:S(2)}, u32[]{:S(2)}) async-start(bf16[128,16,256]{2,1,0:T(8,128)(2,1)} %bitcast.10), calls=%async_computation | async-start | bytes 2097152 | tf_op jit(solution)/shard_map/all_to_all | solution.py:419
  55.8 28.7 %copy-start = (bf16[256,512]{1,0:T(8,128)(2,1)S(1)}, bf16[256,512]{1,0:T(8,128)(2,1)}, u32[]{:S(2)}) copy-start(bf16[256,512]{1,0:T(8,128)(2,1)} %constant.18.clone.time_ref) | copy-start | bytes 786436
  55.8 28.7 %copy-start.1 = (bf16[256,128]{1,0:T(8,128)(2,1)S(1)}, bf16[256,128]{1,0:T(8,128)(2,1)}, u32[]{:S(2)}) copy-start(bf16[256,128]{1,0:T(8,128)(2,1)} %constant.17.clone.plane_ref) | copy-start | bytes 196612
  58.5 26.0 %all-to-all-start.1 = ((bf16[128,8,256]{2,1,0:T(8,128)(2,1)}), bf16[128,8,256]{2,1,0:T(8,128)(2,1)S(1)}, u32[]{:S(2)}, u32[]{:S(2)}) async-start(bf16[128,8,256]{2,1,0:T(8,128)(2,1)} %get-tuple-element.12), calls=%async_computation.1 | async-start | bytes 1048576 | tf_op jit(solution)/shard_map/all_to_all | solution.py:459
  65.0 1.3 %collective-permute-start = (bf16[2,16,8,128]{3,2,1,0:T(8,128)(2,1)S(1)}, bf16[2,16,8,128]{3,2,1,0:T(8,128)(2,1)S(1)}, u32[]{:S(2)}, u32[]{:S(2)}) collective-permute-start(bf16[2,16,8,128]{3,2,1,0:T(8,128)(2,1)S(1)} %get-tuple-element.15), channel_id=1, source_target_pairs={{0,1},{1,0},{2,3},{3,2},{4,5},{5,4},{6,7},{7,6},{8,9},{9,8},{10,11... | collective-permute-start | bytes 196616 | tf_op jit(solution)/shard_map/ppermute | solution.py:460

commit v2 on v1

--- a/solution.py
+++ b/solution.py
@@ -105,10 +105,9 @@
     low = low_lanes((512, 128))
     time_copy.wait()
 
-    def arrive(pair):
-        for g in (2 * pair, 2 * pair + 1):
-            for copy in copies[g]:
-                copy.wait()
+    def arrive(g):
+        for copy in copies[g]:
+            copy.wait()
 
     def activation(g):
         for c in range(4 * g, 4 * g + 4):
@@ -154,19 +153,21 @@
     arrive(0)
     along_time(1, 0)
     activation(0)
+    arrive(1)
     along_time(1, 1)
+    along_time(0, 0)
     activation(1)
     hold(along_y(1))
-    arrive(1)
-    along_time(0, 0)
+    arrive(2)
     along_time(0, 1)
     activation(2)
     first = send(0, along_y(0))
     along_time(1, 2)
+    arrive(3)
     along_time(1, 3)
+    along_time(0, 2)
     activation(3)
     hold(along_y(1))
-    along_time(0, 2)
     along_time(0, 3)
     second = send(1, along_y(0))
     first.wait()
@@ -177,25 +178,17 @@
     def kernel(
         core_ref,
         recv_ref,
-        w_hbm,
+        w_ref,
         xi_ref,
         send_hbm,
         mine_ref,
         other_ref,
-        w_ref,
         back_ref,
         g_ref,
         gr_ref,
         send_ref,
-        loaded,
         sent,
     ):
-        loads = [
-            pltpu.make_async_copy(w_hbm.at[pl.ds(8 * n, 8)], w_ref.at[pl.ds(8 * n, 8)], loaded.at[n])
-            for n in range(2)
-        ]
-        for load in loads:
-            load.start()
         core = core_ref[0]
         line = xi_ref[...].T
         block = recv_ref[...].astype(f32)
@@ -214,8 +207,6 @@
                 other_ref[f, c] = g_ref[f, pl.ds(16 * c + 8 - 8 * core, 8), :].astype(bf16)
         low = low_lanes((16, 128))
         for i in range(16):
-            if i % 8 == 0:
-                loads[i // 8].wait()
             same = jnp.zeros((16, 128), f32)
             cross = jnp.zeros((16, 128), f32)
             for o in range(16):
@@ -305,6 +296,12 @@
     copies[-1].start()
     for copy in copies:
         copy.wait()
+
+
+def fetch_kernel(w_hbm, after_ref, w_ref, sem):
+    copy = pltpu.make_async_copy(w_hbm, w_ref, sem)
+    copy.start()
+    copy.wait()
 
 
 def inverse_kernel(scale_in):
@@ -435,9 +432,18 @@
         name="bypass",
         compiler_params=pltpu.CompilerParams(vmem_limit_bytes=24 << 20),
     )(bypass_weight, local(dz), remote(line))
+    weights = pl.pallas_call(
+        fetch_kernel,
+        in_specs=[hbm, vmem],
+        out_specs=vmem,
+        out_shape=pltpu.VMEM(mode_weight.shape, bf16),
+        scratch_shapes=[pltpu.SemaphoreType.DMA],
+        name="fetch",
+        compiler_params=pltpu.CompilerParams(vmem_limit_bytes=24 << 20),
+    )(remote(mode_weight), local(line))
     rows, mine, other = pl.pallas_call(
         middle_kernel(scale_in, scale_out),
-        in_specs=[pl.BlockSpec(memory_space=pltpu.SMEM), vmem, hbm, vmem],
+        in_specs=[pl.BlockSpec(memory_space=pltpu.SMEM), vmem, vmem, vmem],
         out_specs=[hbm, vmem, vmem],
         out_shape=[
             pltpu.HBM((128, 8, 256), bf16),
@@ -445,17 +451,15 @@
             jax.ShapeDtypeStruct((2, 16, 8, 128), bf16),
         ],
         scratch_shapes=[
-            pltpu.VMEM(mode_weight.shape, bf16),
             pltpu.VMEM((256, 128), bf16),
             pltpu.VMEM((2, 256, 128), f32),
             pltpu.VMEM((256, 128), f32),
             pltpu.VMEM((128, 8, 256), bf16),
             pltpu.SemaphoreType.DMA((2,)),
-            pltpu.SemaphoreType.DMA((2,)),
         ],
         name="middle",
         compiler_params=pltpu.CompilerParams(vmem_limit_bytes=24 << 20),
-    )(core, local(recv), remote(mode_weight), local(line))
+    )(core, local(recv), local(weights), local(line))
     back = lax.all_to_all(rows, "gx", split_axis=0, concat_axis=0, tiled=True)
     theirs = lax.ppermute(other, "sa", [(0, 1), (1, 0)])
     mode_grad = pl.pallas_call(

time: 88.3 us -> 87.3 us (0.989)
  waiting for transfers between devices: 45.4 us -> 44.2 us
    all_to_all x1, waiting for transfers between devices: 27.3 us -> 26.1 us  [shards(): lax.all_to_all(send.reshape(128, 16, 256), 'gx', split_axis=0, concat_axi...]
    pallas_call x0 -> x1, Pallas kernels: none -> 1.24 us  [shards(): pl.pallas_call(fetch_kernel, in_specs=[hbm, vmem], out_specs=vmem, out_sh...]
  transfers between devices with their start and end apart: 3 -> 3, of which waited for: 3 -> 3; matrix products, arithmetic and copies ran while one was open for 0% -> 0% of each run, Pallas kernels for 5% -> 7%
where the time goes in v2:
time: 87.3 us; the launch traced here: 87 us
  waiting for transfers between devices  44.2 us (51%)
  starting transfers between devices  22 us (25%)
  Pallas kernels  20 us (23%)
    all_to_all x1, waiting for transfers between devices, shards(): lax.all_to_all(send.reshape(128, 16, 256), 'gx', split_axis=0, concat_axi...  26.1 us
    all_to_all x1, waiting for transfers between devices, shards(): back = lax.all_to_all(rows, 'gx', split_axis=0, concat_axis=0, tiled=True)  16.9 us
    all_to_all x1, starting transfers between devices, shards(): lax.all_to_all(send.reshape(128, 16, 256), 'gx', split_axis=0, concat_axi...  15.4 us
    pallas_call x1, Pallas kernels, shards(): pl.pallas_call(forward_kernel, in_specs=[hbm] * 5, out_specs=[hbm, vmem],...  8.46 us
    all_to_all x1, starting transfers between devices, shards(): back = lax.all_to_all(rows, 'gx', split_axis=0, concat_axis=0, tiled=True)  6.49 us
    pallas_call x1, Pallas kernels, shards(): pl.pallas_call(inverse_kernel(scale_in), in_specs=[vmem, vmem, vmem, hbm]...  3.52 us
    pallas_call x1, Pallas kernels, shards(): pl.pallas_call(bypass_kernel, in_specs=[vmem, vmem, hbm], out_specs=[hbm,...  3.5 us
    pallas_call x1, Pallas kernels, shards(): pl.pallas_call(middle_kernel(scale_in, scale_out), in_specs=[pl.BlockSpec...  2 us
  transfers between devices with their start and end apart: 3, of which 3 were waited for; matrix products, arithmetic and copies ran while one was open for 0% of the time, Pallas kernels for 7%

profile of v2, /device:TPU:2, one launch (start us, length us, event | category | flops | bytes accessed | tf_op | source)
XLA Modules:
  0.0 87.0 jit_solution(3913894744653752458)
XLA Ops:
  0.6 8.5 %forward.1 = (bf16[64,2,16,256]{3,2,1,0:T(8,128)(2,1)}, bf16[16,4,128,128]{3,2,1,0:T(8,128)(2,1)S(1)}) custom-call(bf16[16,4,128,128]{3,2,1,0:T(8,128)(2,1)} %bitcast.7, bf16[16,4,128,128]{3,2,1,0:T(8,128)(2,1)} %bitcast.8, bf16[16,4,128,128]{3,2,1,0:T(8,128)(2,1)} %bitcast.9, bf16[512,256]{1,0:T(8,128)(2,1)} %constant.14.clone.time_hbm, ...), custom_call_target="tpu_custom_call" | custom-call | tf_op jit(solution)/shard_map/forward/pallas_call | solution.py:390
  9.1 0.0 copy-start.2
  9.1 15.4 %all-to-all-start = ((bf16[128,16,256]{2,1,0:T(8,128)(2,1)}), bf16[128,16,256]{2,1,0:T(8,128)(2,1)S(1)}, u32[]{:S(2)}, u32[]{:S(2)}) async-start(bf16[128,16,256]{2,1,0:T(8,128)(2,1)} %bitcast.10), calls=%async_computation | async-start | bytes 2097152 | tf_op jit(solution)/shard_map/all_to_all | solution.py:416
  24.6 0.0 copy-done.2
  24.6 3.5 %bypass.1 = (f32[16,4,128,128]{3,2,1,0:T(8,128)}, bf16[1024,128]{1,0:T(8,128)(2,1)S(1)}) custom-call(bf16[16,16]{1,0:T(8,128)(2,1)S(1)} %copy-done.2, bf16[16,4,128,128]{3,2,1,0:T(8,128)(2,1)S(1)} %get-tuple-element.10.dz_ref, bf16[1024,128]{1,0:T(8,128)(2,1)} %constant.16.clone.xi_hbm), custom_call_target="tpu_custom_call" | custom-call | tf_op jit(solution)/shard_map/bypass/pallas_call | solution.py:419
  28.1 1.2 %fetch.1.w_ref = bf16[16,16,16,128]{3,2,1,0:T(8,128)(2,1)S(1)} custom-call(bf16[16,16,16,128]{3,2,1,0:T(8,128)(2,1)} %w_hbm.1, bf16[1024,128]{1,0:T(8,128)(2,1)S(1)} %get-tuple-element.11.after_ref.xi_ref), custom_call_target="tpu_custom_call" | custom-call | tf_op jit(solution)/shard_map/fetch/pallas_call | solution.py:435
  29.3 26.1 %all-to-all-done.recv_ref = bf16[128,16,256]{2,1,0:T(8,128)(2,1)S(1)} async-done(((bf16[128,16,256]{2,1,0:T(8,128)(2,1)}), bf16[128,16,256]{2,1,0:T(8,128)(2,1)S(1)}, u32[]{:S(2)}, u32[]{:S(2)}) %all-to-all-start) | async-done | bytes 1048608 | tf_op jit(solution)/shard_map/all_to_all | solution.py:416
  55.4 0.0 copy-start
  55.4 0.0 copy-start.1
  55.4 2.0 %middle.1 = (bf16[128,8,256]{2,1,0:T(8,128)(2,1)}, bf16[2,16,8,128]{3,2,1,0:T(8,128)(2,1)S(1)}, bf16[2,16,8,128]{3,2,1,0:T(8,128)(2,1)S(1)}) custom-call(s32[1]{0:T(128)} %bitcast.core_ref, bf16[128,16,256]{2,1,0:T(8,128)(2,1)S(1)} %all-to-all-done.recv_ref, bf16[16,16,16,128]{3,2,1,0:T(8,128)(2,1)S(1)} %fetch.1.w_ref, ...), custom_call_target="tpu_custom_call" | custom-call | tf_op jit(solution)/shard_map/middle/pallas_call | solution.py:444
  57.4 6.5 %all-to-all-start.1 = ((bf16[128,8,256]{2,1,0:T(8,128)(2,1)}), bf16[128,8,256]{2,1,0:T(8,128)(2,1)S(1)}, u32[]{:S(2)}, u32[]{:S(2)}) async-start(bf16[128,8,256]{2,1,0:T(8,128)(2,1)} %get-tuple-element.12), calls=%async_computation.1 | async-start | bytes 1048576 | tf_op jit(solution)/shard_map/all_to_all | solution.py:463
  63.9 0.1 collective-permute-start
  64.0 1.2 %collective-permute-done.other_ref = bf16[2,16,8,128]{3,2,1,0:T(8,128)(2,1)S(1)} collective-permute-done((bf16[2,16,8,128]{3,2,1,0:T(8,128)(2,1)S(1)}, bf16[2,16,8,128]{3,2,1,0:T(8,128)(2,1)S(1)}, u32[]{:S(2)}, u32[]{:S(2)}) %collective-permute-start) | collective-permute-done | bytes 65568 | tf_op jit(solution)/shard_map/ppermute | solution.py:464
  65.2 1.3 %modes.1 = f32[16,16,8,128]{3,2,1,0:T(8,128)} custom-call(bf16[2,16,8,128]{3,2,1,0:T(8,128)(2,1)S(1)} %get-tuple-element.14.mine_ref, bf16[2,16,8,128]{3,2,1,0:T(8,128)(2,1)S(1)} %collective-permute-done.other_ref), custom_call_target="tpu_custom_call" | custom-call | tf_op jit(solution)/shard_map/modes/pallas_call | solution.py:465
  66.6 16.9 %all-to-all-done.1.recv_ref = bf16[128,8,256]{2,1,0:T(8,128)(2,1)S(1)} async-done(((bf16[128,8,256]{2,1,0:T(8,128)(2,1)}), bf16[128,8,256]{2,1,0:T(8,128)(2,1)S(1)}, u32[]{:S(2)}, u32[]{:S(2)}) %all-to-all-start.1) | async-done | bytes 524320 | tf_op jit(solution)/shard_map/all_to_all | solution.py:463
  83.5 0.0 copy-done
  83.5 0.0 copy-done.1
  83.5 3.5 %inverse.1 = bf16[16,4,128,128]{3,2,1,0:T(8,128)(2,1)} custom-call(bf16[128,8,256]{2,1,0:T(8,128)(2,1)S(1)} %all-to-all-done.1.recv_ref, bf16[256,128]{1,0:T(8,128)(2,1)S(1)} %copy-done.1, bf16[256,512]{1,0:T(8,128)(2,1)S(1)} %copy-done, f32[16,4,128,128]{3,2,1,0:T(8,128)} %get-tuple-element.13.bypass_hbm), custom_call_target="tpu_custom_call" | custom-call | tf_op jit(solution)/shard_map/inverse/pallas_call | solution.py:474
Async XLA Ops:
  9.1 15.5 %copy-start.2 = (bf16[16,16]{1,0:T(8,128)(2,1)S(1)}, bf16[16,16]{1,0:T(8,128)(2,1)}, u32[]{:S(2)}) copy-start(bf16[16,16]{1,0:T(8,128)(2,1)} %b_ref.1) | copy-start | bytes 1540
  9.1 46.3 %all-to-all-start = ((bf16[128,16,256]{2,1,0:T(8,128)(2,1)}), bf16[128,16,256]{2,1,0:T(8,128)(2,1)S(1)}, u32[]{:S(2)}, u32[]{:S(2)}) async-start(bf16[128,16,256]{2,1,0:T(8,128)(2,1)} %bitcast.10), calls=%async_computation | async-start | bytes 2097152 | tf_op jit(solution)/shard_map/all_to_all | solution.py:416
  55.4 28.1 %copy-start = (bf16[256,512]{1,0:T(8,128)(2,1)S(1)}, bf16[256,512]{1,0:T(8,128)(2,1)}, u32[]{:S(2)}) copy-start(bf16[256,512]{1,0:T(8,128)(2,1)} %constant.18.clone.time_ref) | copy-start | bytes 786436
  55.4 28.1 %copy-start.1 = (bf16[256,128]{1,0:T(8,128)(2,1)S(1)}, bf16[256,128]{1,0:T(8,128)(2,1)}, u32[]{:S(2)}) copy-start(bf16[256,128]{1,0:T(8,128)(2,1)} %constant.17.clone.plane_ref) | copy-start | bytes 196612
  57.4 26.1 %all-to-all-start.1 = ((bf16[128,8,256]{2,1,0:T(8,128)(2,1)}), bf16[128,8,256]{2,1,0:T(8,128)(2,1)S(1)}, u32[]{:S(2)}, u32[]{:S(2)}) async-start(bf16[128,8,256]{2,1,0:T(8,128)(2,1)} %get-tuple-element.12), calls=%async_computation.1 | async-start | bytes 1048576 | tf_op jit(solution)/shard_map/all_to_all | solution.py:463
  63.9 1.3 %collective-permute-start = (bf16[2,16,8,128]{3,2,1,0:T(8,128)(2,1)S(1)}, bf16[2,16,8,128]{3,2,1,0:T(8,128)(2,1)S(1)}, u32[]{:S(2)}, u32[]{:S(2)}) collective-permute-start(bf16[2,16,8,128]{3,2,1,0:T(8,128)(2,1)S(1)} %get-tuple-element.15), channel_id=1, source_target_pairs={{0,1},{1,0},{2,3},{3,2},{4,5},{5,4},{6,7},{7,6},{8,9},{9,8},{10,11... | collective-permute-start | bytes 196616 | tf_op jit(solution)/shard_map/ppermute | solution.py:464

commit v3 on v2

--- a/solution.py
+++ b/solution.py
@@ -40,8 +40,8 @@
     time_forward = np.einsum("cd,qhkt->ctqhdk", four, time).reshape(4 * cells_time, -1)
     time_inverse = np.einsum("cd,qhkt->qhckdt", four, time).reshape(-1, 4 * cells_time)
     plane = np.block([[cy, sy], [-sy, cy]])
-    plane_rows = plane.reshape(2, MY, 1, -1).repeat(slab, 2).transpose(1, 2, 0, 3)
-    plane_rows = plane_rows.reshape(MY * slab * 2, -1)
+    plane_rows = plane.reshape(2, MY, 1, -1).repeat(2, 2).transpose(1, 2, 0, 3)
+    plane_rows = plane_rows.reshape(MY * 4, -1)
     line = np.stack([np.concatenate([cx, -sx]), np.concatenate([sx, cx])], -1)
     line = line.reshape(2 * modes_x, -1).T
     return [
@@ -97,12 +97,13 @@
         for copy in trio:
             copy.start()
         copies.append(trio)
-    row_x = lax.broadcasted_iota(jnp.int32, (512, 256), 0) // 2 % 4
+    row_x = lax.broadcasted_iota(jnp.int32, (256, 256), 0) // 2 % 2
     plane_copy.wait()
     plane = plane_ref[...].astype(f32)
-    for x in range(4):
+    for x in range(2):
         table_ref[:, 256 * x : 256 * x + 256] = jnp.where(row_x == x, plane, 0.0).astype(bf16)
-    low = low_lanes((512, 128))
+    top = lax.broadcasted_iota(jnp.int32, (32, 8, 128), 1) < 4
+    low = low_lanes((256, 128))
     time_copy.wait()
 
     def arrive(g):
@@ -130,12 +131,27 @@
                 ] = sect[128 * x : 128 * x + 128, 128 * q : 128 * q + 128]
 
     def along_y(field):
-        spectra = jnp.dot(table_ref[...], sect_ref[field], preferred_element_type=f32)
-        first, second = spectra[:, :128], spectra[:, 128:]
-        return (
-            jnp.where(low, first, pltpu.roll(second, 64, 1)).reshape(64, 8, 128),
-            jnp.where(low, pltpu.roll(first, 64, 1), second).reshape(64, 8, 128),
-        )
+        parts = []
+        for pair in range(2):
+            spectra = jnp.dot(
+                table_ref[...],
+                sect_ref[field, 512 * pair : 512 * pair + 512, :],
+                preferred_element_type=f32,
+            )
+            first, second = spectra[:, :128], spectra[:, 128:]
+            parts.append(
+                (
+                    jnp.where(low, first, pltpu.roll(second, 64, 1)).reshape(32, 8, 128),
+                    jnp.where(low, pltpu.roll(first, 64, 1), second).reshape(32, 8, 128),
+                )
+            )
+        halves = []
+        for h in range(2):
+            one, two = parts[0][h], parts[1][h]
+            even = jnp.where(top, one, pltpu.roll(two, 4, 1))
+            odd = jnp.where(top, pltpu.roll(one, 4, 1), two)
+            halves.append(jnp.stack([even, odd], axis=1).reshape(64, 8, 128))
+        return halves
 
     def hold(halves):
         for h in range(2):
@@ -150,20 +166,18 @@
         copy.start()
         return copy
 
-    arrive(0)
+    for g in range(4):
+        arrive(g)
     along_time(1, 0)
     activation(0)
-    arrive(1)
     along_time(1, 1)
     along_time(0, 0)
     activation(1)
     hold(along_y(1))
-    arrive(2)
     along_time(0, 1)
     activation(2)
     first = send(0, along_y(0))
     along_time(1, 2)
-    arrive(3)
     along_time(1, 3)
     along_time(0, 2)
     activation(3)
@@ -397,7 +411,7 @@
             pltpu.VMEM(time_forward.shape, bf16),
             pltpu.VMEM(plane.shape, bf16),
             pltpu.VMEM((64, 2, 16, 256), bf16),
-            pltpu.VMEM((512, 1024), bf16),
+            pltpu.VMEM((256, 512), bf16),
             pltpu.VMEM((2, 1024, 256), bf16),
             pltpu.VMEM((2, 64, 8, 128), f32),
             pltpu.SemaphoreType.DMA((3, 4)),

time: 87.3 us -> 86.4 us (0.990)
  Pallas kernels: 20 us -> 19.1 us
    pallas_call x1, Pallas kernels: 8.46 us -> 7.53 us  [shards(): pl.pallas_call(forward_kernel, in_specs=[hbm] * 5, out_specs=[hbm, vmem],...]
where the time goes in v3:
time: 86.4 us; the launch traced here: 86.1 us
  waiting for transfers between devices  44.2 us (51%)
  starting transfers between devices  22 us (25%)
  Pallas kernels  19.1 us (22%)
    all_to_all x1, waiting for transfers between devices, shards(): lax.all_to_all(send.reshape(128, 16, 256), 'gx', split_axis=0, concat_axi...  26.1 us
    all_to_all x1, waiting for transfers between devices, shards(): back = lax.all_to_all(rows, 'gx', split_axis=0, concat_axis=0, tiled=True)  16.9 us
    all_to_all x1, starting transfers between devices, shards(): lax.all_to_all(send.reshape(128, 16, 256), 'gx', split_axis=0, concat_axi...  15.4 us
    pallas_call x1, Pallas kernels, shards(): pl.pallas_call(forward_kernel, in_specs=[hbm] * 5, out_specs=[hbm, vmem],...  7.53 us
    all_to_all x1, starting transfers between devices, shards(): back = lax.all_to_all(rows, 'gx', split_axis=0, concat_axis=0, tiled=True)  6.49 us
    pallas_call x1, Pallas kernels, shards(): pl.pallas_call(inverse_kernel(scale_in), in_specs=[vmem, vmem, vmem, hbm]...  3.52 us
    pallas_call x1, Pallas kernels, shards(): pl.pallas_call(bypass_kernel, in_specs=[vmem, vmem, hbm], out_specs=[hbm,...  3.5 us
    pallas_call x1, Pallas kernels, shards(): pl.pallas_call(middle_kernel(scale_in, scale_out), in_specs=[pl.BlockSpec...  2.01 us
  transfers between devices with their start and end apart: 3, of which 3 were waited for; matrix products, arithmetic and copies ran while one was open for 0% of the time, Pallas kernels for 7%

profile of v3, /device:TPU:2, one launch (start us, length us, event | category | flops | bytes accessed | tf_op | source)
XLA Modules:
  0.0 86.1 jit_solution(12262332149998719957)
XLA Ops:
  0.6 7.5 %forward.1 = (bf16[64,2,16,256]{3,2,1,0:T(8,128)(2,1)}, bf16[16,4,128,128]{3,2,1,0:T(8,128)(2,1)S(1)}) custom-call(bf16[16,4,128,128]{3,2,1,0:T(8,128)(2,1)} %bitcast.6, bf16[16,4,128,128]{3,2,1,0:T(8,128)(2,1)} %bitcast.7, bf16[16,4,128,128]{3,2,1,0:T(8,128)(2,1)} %bitcast.8, bf16[512,256]{1,0:T(8,128)(2,1)} %constant.14.clone.time_hbm, ...), custom_call_target="tpu_custom_call" | custom-call | tf_op jit(solution)/shard_map/forward/pallas_call | solution.py:404
  8.2 0.0 copy-start.2
  8.2 15.4 %all-to-all-start = ((bf16[128,16,256]{2,1,0:T(8,128)(2,1)}), bf16[128,16,256]{2,1,0:T(8,128)(2,1)S(1)}, u32[]{:S(2)}, u32[]{:S(2)}) async-start(bf16[128,16,256]{2,1,0:T(8,128)(2,1)} %bitcast.10), calls=%async_computation | async-start | bytes 2097152 | tf_op jit(solution)/shard_map/all_to_all | solution.py:430
  23.6 0.0 copy-done.2
  23.6 3.5 %bypass.1 = (f32[16,4,128,128]{3,2,1,0:T(8,128)}, bf16[1024,128]{1,0:T(8,128)(2,1)S(1)}) custom-call(bf16[16,16]{1,0:T(8,128)(2,1)S(1)} %copy-done.2, bf16[16,4,128,128]{3,2,1,0:T(8,128)(2,1)S(1)} %get-tuple-element.10.dz_ref, bf16[1024,128]{1,0:T(8,128)(2,1)} %constant.16.clone.xi_hbm), custom_call_target="tpu_custom_call" | custom-call | tf_op jit(solution)/shard_map/bypass/pallas_call | solution.py:433
  27.2 1.2 %fetch.1.w_ref = bf16[16,16,16,128]{3,2,1,0:T(8,128)(2,1)S(1)} custom-call(bf16[16,16,16,128]{3,2,1,0:T(8,128)(2,1)} %w_hbm.1, bf16[1024,128]{1,0:T(8,128)(2,1)S(1)} %get-tuple-element.11.after_ref.xi_ref), custom_call_target="tpu_custom_call" | custom-call | tf_op jit(solution)/shard_map/fetch/pallas_call | solution.py:449
  28.4 26.1 %all-to-all-done.recv_ref = bf16[128,16,256]{2,1,0:T(8,128)(2,1)S(1)} async-done(((bf16[128,16,256]{2,1,0:T(8,128)(2,1)}), bf16[128,16,256]{2,1,0:T(8,128)(2,1)S(1)}, u32[]{:S(2)}, u32[]{:S(2)}) %all-to-all-start) | async-done | bytes 1048608 | tf_op jit(solution)/shard_map/all_to_all | solution.py:430
  54.5 0.0 copy-start
  54.5 0.0 copy-start.1
  54.5 2.0 %middle.1 = (bf16[128,8,256]{2,1,0:T(8,128)(2,1)}, bf16[2,16,8,128]{3,2,1,0:T(8,128)(2,1)S(1)}, bf16[2,16,8,128]{3,2,1,0:T(8,128)(2,1)S(1)}) custom-call(s32[1]{0:T(128)} %bitcast.core_ref, bf16[128,16,256]{2,1,0:T(8,128)(2,1)S(1)} %all-to-all-done.recv_ref, bf16[16,16,16,128]{3,2,1,0:T(8,128)(2,1)S(1)} %fetch.1.w_ref, ...), custom_call_target="tpu_custom_call" | custom-call | tf_op jit(solution)/shard_map/middle/pallas_call | solution.py:458
  56.5 6.5 %all-to-all-start.1 = ((bf16[128,8,256]{2,1,0:T(8,128)(2,1)}), bf16[128,8,256]{2,1,0:T(8,128)(2,1)S(1)}, u32[]{:S(2)}, u32[]{:S(2)}) async-start(bf16[128,8,256]{2,1,0:T(8,128)(2,1)} %get-tuple-element.12), calls=%async_computation.1 | async-start | bytes 1048576 | tf_op jit(solution)/shard_map/all_to_all | solution.py:477
  63.0 0.1 collective-permute-start
  63.1 1.2 %collective-permute-done.other_ref = bf16[2,16,8,128]{3,2,1,0:T(8,128)(2,1)S(1)} collective-permute-done((bf16[2,16,8,128]{3,2,1,0:T(8,128)(2,1)S(1)}, bf16[2,16,8,128]{3,2,1,0:T(8,128)(2,1)S(1)}, u32[]{:S(2)}, u32[]{:S(2)}) %collective-permute-start) | collective-permute-done | bytes 65568 | tf_op jit(solution)/shard_map/ppermute | solution.py:478
  64.3 1.3 %modes.1 = f32[16,16,8,128]{3,2,1,0:T(8,128)} custom-call(bf16[2,16,8,128]{3,2,1,0:T(8,128)(2,1)S(1)} %get-tuple-element.14.mine_ref, bf16[2,16,8,128]{3,2,1,0:T(8,128)(2,1)S(1)} %collective-permute-done.other_ref), custom_call_target="tpu_custom_call" | custom-call | tf_op jit(solution)/shard_map/modes/pallas_call | solution.py:479
  65.6 16.9 %all-to-all-done.1.recv_ref = bf16[128,8,256]{2,1,0:T(8,128)(2,1)S(1)} async-done(((bf16[128,8,256]{2,1,0:T(8,128)(2,1)}), bf16[128,8,256]{2,1,0:T(8,128)(2,1)S(1)}, u32[]{:S(2)}, u32[]{:S(2)}) %all-to-all-start.1) | async-done | bytes 524320 | tf_op jit(solution)/shard_map/all_to_all | solution.py:477
  82.5 0.0 copy-done
  82.5 0.0 copy-done.1
  82.5 3.5 %inverse.1 = bf16[16,4,128,128]{3,2,1,0:T(8,128)(2,1)} custom-call(bf16[128,8,256]{2,1,0:T(8,128)(2,1)S(1)} %all-to-all-done.1.recv_ref, bf16[256,128]{1,0:T(8,128)(2,1)S(1)} %copy-done.1, bf16[256,512]{1,0:T(8,128)(2,1)S(1)} %copy-done, f32[16,4,128,128]{3,2,1,0:T(8,128)} %get-tuple-element.13.bypass_hbm), custom_call_target="tpu_custom_call" | custom-call | tf_op jit(solution)/shard_map/inverse/pallas_call | solution.py:488
Async XLA Ops:
  8.2 15.5 %copy-start.2 = (bf16[16,16]{1,0:T(8,128)(2,1)S(1)}, bf16[16,16]{1,0:T(8,128)(2,1)}, u32[]{:S(2)}) copy-start(bf16[16,16]{1,0:T(8,128)(2,1)} %b_ref.1) | copy-start | bytes 1540
  8.2 46.3 %all-to-all-start = ((bf16[128,16,256]{2,1,0:T(8,128)(2,1)}), bf16[128,16,256]{2,1,0:T(8,128)(2,1)S(1)}, u32[]{:S(2)}, u32[]{:S(2)}) async-start(bf16[128,16,256]{2,1,0:T(8,128)(2,1)} %bitcast.10), calls=%async_computation | async-start | bytes 2097152 | tf_op jit(solution)/shard_map/all_to_all | solution.py:430
  54.5 28.1 %copy-start = (bf16[256,512]{1,0:T(8,128)(2,1)S(1)}, bf16[256,512]{1,0:T(8,128)(2,1)}, u32[]{:S(2)}) copy-start(bf16[256,512]{1,0:T(8,128)(2,1)} %constant.18.clone.time_ref) | copy-start | bytes 786436
  54.5 28.1 %copy-start.1 = (bf16[256,128]{1,0:T(8,128)(2,1)S(1)}, bf16[256,128]{1,0:T(8,128)(2,1)}, u32[]{:S(2)}) copy-start(bf16[256,128]{1,0:T(8,128)(2,1)} %constant.17.clone.plane_ref) | copy-start | bytes 196612
  56.5 26.0 %all-to-all-start.1 = ((bf16[128,8,256]{2,1,0:T(8,128)(2,1)}), bf16[128,8,256]{2,1,0:T(8,128)(2,1)S(1)}, u32[]{:S(2)}, u32[]{:S(2)}) async-start(bf16[128,8,256]{2,1,0:T(8,128)(2,1)} %get-tuple-element.12), calls=%async_computation.1 | async-start | bytes 1048576 | tf_op jit(solution)/shard_map/all_to_all | solution.py:477
  63.0 1.3 %collective-permute-start = (bf16[2,16,8,128]{3,2,1,0:T(8,128)(2,1)S(1)}, bf16[2,16,8,128]{3,2,1,0:T(8,128)(2,1)S(1)}, u32[]{:S(2)}, u32[]{:S(2)}) collective-permute-start(bf16[2,16,8,128]{3,2,1,0:T(8,128)(2,1)S(1)} %get-tuple-element.15), channel_id=1, source_target_pairs={{0,1},{1,0},{2,3},{3,2},{4,5},{5,4},{6,7},{7,6},{8,9},{9,8},{10,11... | collective-permute-start | bytes 196616 | tf_op jit(solution)/shard_map/ppermute | solution.py:478

commit v4 on v3

--- a/solution.py
+++ b/solution.py
@@ -318,7 +318,7 @@
     copy.wait()
 
 
-def inverse_kernel(scale_in):
+def inverse_kernel():
     def kernel(recv_ref, plane_ref, time_ref, bypass_hbm, out_hbm, rows_ref, bypass_ref, out_ref, loads, sems):
         arriving = [
             pltpu.make_async_copy(bypass_hbm.at[:, x], bypass_ref.at[:, x], loads.at[x])
@@ -363,7 +363,7 @@
             for g in range(4):
                 for c in range(4):
                     out_ref[4 * g + c, x] = (
-                        scale_in * spectral[128 * g : 128 * g + 128, 128 * c : 128 * c + 128]
+                        spectral[128 * g : 128 * g + 128, 128 * c : 128 * c + 128]
                         + bypass_ref[4 * g + c, x]
                     ).astype(bf16)
             copies.append(
@@ -396,6 +396,8 @@
     time_forward, time_inverse, plane, plane_back, line = constants(
         cells_x, cells_y, cells_time, modes_x, slab
     )
+    assert math.frexp(scale_in)[0] == 0.5
+    time_inverse = (time_inverse.astype(np.float32) * scale_in).astype(bf16)
     core = lax.axis_index("sa").astype(jnp.int32).reshape(1)
 
     vmem = pl.BlockSpec(memory_space=pltpu.VMEM)
@@ -486,7 +488,7 @@
         compiler_params=pltpu.CompilerParams(vmem_limit_bytes=24 << 20),
     )(local(mine), local(theirs))
     input_grad = pl.pallas_call(
-        inverse_kernel(scale_in),
+        inverse_kernel(),
         in_specs=[vmem, vmem, vmem, hbm],
         out_specs=hbm,
         out_shape=jax.ShapeDtypeStruct(field, bf16),

time: 86.4 us -> 86.3 us (level)
  no operation moved by 1% of the time
where the time goes in v4:
time: 86.3 us; the launch traced here: 86.1 us
  waiting for transfers between devices  44.2 us (51%)
  starting transfers between devices  22 us (25%)
  Pallas kernels  19.1 us (22%)
    all_to_all x1, waiting for transfers between devices, shards(): lax.all_to_all(send.reshape(128, 16, 256), 'gx', split_axis=0, concat_axi...  26.1 us
    all_to_all x1, waiting for transfers between devices, shards(): back = lax.all_to_all(rows, 'gx', split_axis=0, concat_axis=0, tiled=True)  16.9 us
    all_to_all x1, starting transfers between devices, shards(): lax.all_to_all(send.reshape(128, 16, 256), 'gx', split_axis=0, concat_axi...  15.4 us
    pallas_call x1, Pallas kernels, shards(): pl.pallas_call(forward_kernel, in_specs=[hbm] * 5, out_specs=[hbm, vmem],...  7.53 us
    all_to_all x1, starting transfers between devices, shards(): back = lax.all_to_all(rows, 'gx', split_axis=0, concat_axis=0, tiled=True)  6.49 us
    pallas_call x1, Pallas kernels, shards(): pl.pallas_call(inverse_kernel(), in_specs=[vmem, vmem, vmem, hbm], out_sp...  3.51 us
    pallas_call x1, Pallas kernels, shards(): pl.pallas_call(bypass_kernel, in_specs=[vmem, vmem, hbm], out_specs=[hbm,...  3.5 us
    pallas_call x1, Pallas kernels, shards(): pl.pallas_call(middle_kernel(scale_in, scale_out), in_specs=[pl.BlockSpec...  2.01 us
  transfers between devices with their start and end apart: 3, of which 3 were waited for; matrix products, arithmetic and copies ran while one was open for 0% of the time, Pallas kernels for 7%

profile of v4, /device:TPU:2, one launch (start us, length us, event | category | flops | bytes accessed | tf_op | source)
XLA Modules:
  0.0 86.1 jit_solution(17864812909877595912)
XLA Ops:
  0.6 7.5 %forward.1 = (bf16[64,2,16,256]{3,2,1,0:T(8,128)(2,1)}, bf16[16,4,128,128]{3,2,1,0:T(8,128)(2,1)S(1)}) custom-call(bf16[16,4,128,128]{3,2,1,0:T(8,128)(2,1)} %bitcast.6, bf16[16,4,128,128]{3,2,1,0:T(8,128)(2,1)} %bitcast.7, bf16[16,4,128,128]{3,2,1,0:T(8,128)(2,1)} %bitcast.8, bf16[512,256]{1,0:T(8,128)(2,1)} %constant.14.clone.time_hbm, ...), custom_call_target="tpu_custom_call" | custom-call | tf_op jit(solution)/shard_map/forward/pallas_call | solution.py:406
  8.2 0.0 copy-start.2
  8.2 15.4 %all-to-all-start = ((bf16[128,16,256]{2,1,0:T(8,128)(2,1)}), bf16[128,16,256]{2,1,0:T(8,128)(2,1)S(1)}, u32[]{:S(2)}, u32[]{:S(2)}) async-start(bf16[128,16,256]{2,1,0:T(8,128)(2,1)} %bitcast.10), calls=%async_computation | async-start | bytes 2097152 | tf_op jit(solution)/shard_map/all_to_all | solution.py:432
  23.6 0.0 copy-done.2
  23.6 3.5 %bypass.1 = (f32[16,4,128,128]{3,2,1,0:T(8,128)}, bf16[1024,128]{1,0:T(8,128)(2,1)S(1)}) custom-call(bf16[16,16]{1,0:T(8,128)(2,1)S(1)} %copy-done.2, bf16[16,4,128,128]{3,2,1,0:T(8,128)(2,1)S(1)} %get-tuple-element.10.dz_ref, bf16[1024,128]{1,0:T(8,128)(2,1)} %constant.16.clone.xi_hbm), custom_call_target="tpu_custom_call" | custom-call | tf_op jit(solution)/shard_map/bypass/pallas_call | solution.py:435
  27.2 1.2 %fetch.1.w_ref = bf16[16,16,16,128]{3,2,1,0:T(8,128)(2,1)S(1)} custom-call(bf16[16,16,16,128]{3,2,1,0:T(8,128)(2,1)} %w_hbm.1, bf16[1024,128]{1,0:T(8,128)(2,1)S(1)} %get-tuple-element.11.after_ref.xi_ref), custom_call_target="tpu_custom_call" | custom-call | tf_op jit(solution)/shard_map/fetch/pallas_call | solution.py:451
  28.4 26.1 %all-to-all-done.recv_ref = bf16[128,16,256]{2,1,0:T(8,128)(2,1)S(1)} async-done(((bf16[128,16,256]{2,1,0:T(8,128)(2,1)}), bf16[128,16,256]{2,1,0:T(8,128)(2,1)S(1)}, u32[]{:S(2)}, u32[]{:S(2)}) %all-to-all-start) | async-done | bytes 1048608 | tf_op jit(solution)/shard_map/all_to_all | solution.py:432
  54.5 0.0 copy-start
  54.5 0.0 copy-start.1
  54.5 2.0 %middle.1 = (bf16[128,8,256]{2,1,0:T(8,128)(2,1)}, bf16[2,16,8,128]{3,2,1,0:T(8,128)(2,1)S(1)}, bf16[2,16,8,128]{3,2,1,0:T(8,128)(2,1)S(1)}) custom-call(s32[1]{0:T(128)} %bitcast.core_ref, bf16[128,16,256]{2,1,0:T(8,128)(2,1)S(1)} %all-to-all-done.recv_ref, bf16[16,16,16,128]{3,2,1,0:T(8,128)(2,1)S(1)} %fetch.1.w_ref, ...), custom_call_target="tpu_custom_call" | custom-call | tf_op jit(solution)/shard_map/middle/pallas_call | solution.py:460
  56.5 6.5 %all-to-all-start.1 = ((bf16[128,8,256]{2,1,0:T(8,128)(2,1)}), bf16[128,8,256]{2,1,0:T(8,128)(2,1)S(1)}, u32[]{:S(2)}, u32[]{:S(2)}) async-start(bf16[128,8,256]{2,1,0:T(8,128)(2,1)} %get-tuple-element.12), calls=%async_computation.1 | async-start | bytes 1048576 | tf_op jit(solution)/shard_map/all_to_all | solution.py:479
  63.0 0.1 collective-permute-start
  63.1 1.2 %collective-permute-done.other_ref = bf16[2,16,8,128]{3,2,1,0:T(8,128)(2,1)S(1)} collective-permute-done((bf16[2,16,8,128]{3,2,1,0:T(8,128)(2,1)S(1)}, bf16[2,16,8,128]{3,2,1,0:T(8,128)(2,1)S(1)}, u32[]{:S(2)}, u32[]{:S(2)}) %collective-permute-start) | collective-permute-done | bytes 65568 | tf_op jit(solution)/shard_map/ppermute | solution.py:480
  64.3 1.3 %modes.1 = f32[16,16,8,128]{3,2,1,0:T(8,128)} custom-call(bf16[2,16,8,128]{3,2,1,0:T(8,128)(2,1)S(1)} %get-tuple-element.14.mine_ref, bf16[2,16,8,128]{3,2,1,0:T(8,128)(2,1)S(1)} %collective-permute-done.other_ref), custom_call_target="tpu_custom_call" | custom-call | tf_op jit(solution)/shard_map/modes/pallas_call | solution.py:481
  65.6 16.9 %all-to-all-done.1.recv_ref = bf16[128,8,256]{2,1,0:T(8,128)(2,1)S(1)} async-done(((bf16[128,8,256]{2,1,0:T(8,128)(2,1)}), bf16[128,8,256]{2,1,0:T(8,128)(2,1)S(1)}, u32[]{:S(2)}, u32[]{:S(2)}) %all-to-all-start.1) | async-done | bytes 524320 | tf_op jit(solution)/shard_map/all_to_all | solution.py:479
  82.5 0.0 copy-done
  82.5 0.0 copy-done.1
  82.5 3.5 %inverse.1 = bf16[16,4,128,128]{3,2,1,0:T(8,128)(2,1)} custom-call(bf16[128,8,256]{2,1,0:T(8,128)(2,1)S(1)} %all-to-all-done.1.recv_ref, bf16[256,128]{1,0:T(8,128)(2,1)S(1)} %copy-done.1, bf16[256,512]{1,0:T(8,128)(2,1)S(1)} %copy-done, f32[16,4,128,128]{3,2,1,0:T(8,128)} %get-tuple-element.13.bypass_hbm), custom_call_target="tpu_custom_call" | custom-call | tf_op jit(solution)/shard_map/inverse/pallas_call | solution.py:490
Async XLA Ops:
  8.2 15.5 %copy-start.2 = (bf16[16,16]{1,0:T(8,128)(2,1)S(1)}, bf16[16,16]{1,0:T(8,128)(2,1)}, u32[]{:S(2)}) copy-start(bf16[16,16]{1,0:T(8,128)(2,1)} %b_ref.1) | copy-start | bytes 1540
  8.2 46.3 %all-to-all-start = ((bf16[128,16,256]{2,1,0:T(8,128)(2,1)}), bf16[128,16,256]{2,1,0:T(8,128)(2,1)S(1)}, u32[]{:S(2)}, u32[]{:S(2)}) async-start(bf16[128,16,256]{2,1,0:T(8,128)(2,1)} %bitcast.10), calls=%async_computation | async-start | bytes 2097152 | tf_op jit(solution)/shard_map/all_to_all | solution.py:432
  54.5 28.1 %copy-start = (bf16[256,512]{1,0:T(8,128)(2,1)S(1)}, bf16[256,512]{1,0:T(8,128)(2,1)}, u32[]{:S(2)}) copy-start(bf16[256,512]{1,0:T(8,128)(2,1)} %constant.18.clone.time_ref) | copy-start | bytes 786436
  54.5 28.1 %copy-start.1 = (bf16[256,128]{1,0:T(8,128)(2,1)S(1)}, bf16[256,128]{1,0:T(8,128)(2,1)}, u32[]{:S(2)}) copy-start(bf16[256,128]{1,0:T(8,128)(2,1)} %constant.17.clone.plane_ref) | copy-start | bytes 196612
  56.5 26.0 %all-to-all-start.1 = ((bf16[128,8,256]{2,1,0:T(8,128)(2,1)}), bf16[128,8,256]{2,1,0:T(8,128)(2,1)S(1)}, u32[]{:S(2)}, u32[]{:S(2)}) async-start(bf16[128,8,256]{2,1,0:T(8,128)(2,1)} %get-tuple-element.12), calls=%async_computation.1 | async-start | bytes 1048576 | tf_op jit(solution)/shard_map/all_to_all | solution.py:479
  63.0 1.3 %collective-permute-start = (bf16[2,16,8,128]{3,2,1,0:T(8,128)(2,1)S(1)}, bf16[2,16,8,128]{3,2,1,0:T(8,128)(2,1)S(1)}, u32[]{:S(2)}, u32[]{:S(2)}) collective-permute-start(bf16[2,16,8,128]{3,2,1,0:T(8,128)(2,1)S(1)} %get-tuple-element.15), channel_id=1, source_target_pairs={{0,1},{1,0},{2,3},{3,2},{4,5},{5,4},{6,7},{7,6},{8,9},{9,8},{10,11... | collective-permute-start | bytes 196616 | tf_op jit(solution)/shard_map/ppermute | solution.py:480
